TPU v7x, 512 devices: a whole 4x8x8 slice. The times are simulated.
512 devices in a mesh: lat: 64 (over z, x, core), rad: 8 (over y).
Axes of the slice: x: 4, y: 8, z: 8, core: 2. Of those that a mesh axis runs over, the one named last changes fastest.
Arguments:
- fourier: bfloat16 [2, 2, 256, 2, 64, 1152], P(None, None, 'rad', None, None, 'lat'), may hold values from -6 to 6
- legendre: bfloat16 [64, 1024, 1152], P('lat'), may hold values from -0.1875 to 0.1875
- inverse: bfloat16 [1024, 512, 512], P('lat', 'rad'), may hold values from -0.25 to 0.25
- order_of_slot: int32 [64], replicated, may hold values from 0 to 63, each once
- degree_of_slot: int32 [1024], replicated, may hold values from 0 to 1023, each once
- degree_count: int32 [64], replicated, may hold values from 1 to 1024, as said below
Outputs:
- solved: float32 [1024, 512, 2, 64], P('lat', 'rad')
Inputs may be any that keep to these rules, and one draw needn't show every extreme that they name: `order_of_slot`: a permutation; the index p of lat is given slot p. `degree_of_slot`: a permutation; the index p of lat is given slots p * 16 to (p + 1) * 16 - 1. Order k is live on the last degree_count[k] degrees of the band; some order has all 1024.
All inputs are finite; a program needn't handle non-finite values.
Results may differ from a plain program's by a relative error of at most 0.0042.
Values may be sent and summed in bfloat16 or wider, within the bound.
A program may use at most 64 MiB of HBM per device.

v0:
```python
import jax
import jax.numpy as jnp
from jax import lax
from jax.sharding import PartitionSpec as P


def analyze(received, legendre, first_live):
    north_rows = received[:, :, :, 0].astype(jnp.float32)
    south_rows = received[:, :, :, 1].astype(jnp.float32)
    even_part = (north_rows + south_rows).astype(jnp.bfloat16)
    odd_part = (north_rows - south_rows).astype(jnp.bfloat16)
    slot_count = legendre.shape[0]
    band_size = legendre.shape[1]
    band_index = lax.broadcasted_iota(jnp.int32, (slot_count, band_size), 1)
    live_mask = band_index >= first_live[:, None]
    use_even = (band_index - first_live[:, None]) % 2 == 0
    full_even = jnp.einsum(
        "ojn,fcron->ojfcr", legendre, even_part, preferred_element_type=jnp.float32
    )
    full_odd = jnp.einsum(
        "ojn,fcron->ojfcr", legendre, odd_part, preferred_element_type=jnp.float32
    )
    chosen = jnp.where(use_even[:, :, None, None, None], full_even, full_odd)
    return jnp.where(live_mask[:, :, None, None, None], chosen, 0.0).astype(jnp.bfloat16)


def on_device(fourier, legendre, inverse, order_of_slot, degree_of_slot, degree_count):
    slot_count = legendre.shape[0]
    band_size = legendre.shape[1]
    lat_index = lax.axis_index("lat")
    my_orders = lax.dynamic_slice_in_dim(order_of_slot, lat_index * slot_count, slot_count)
    first_live = band_size - jnp.take(degree_count, my_orders)
    picked = jnp.take(fourier, order_of_slot, axis=4)
    received = lax.all_to_all(picked, "lat", split_axis=4, concat_axis=5, tiled=True)
    coefficients = analyze(received, legendre, first_live)
    by_degree = jnp.take(coefficients, degree_of_slot, axis=1)
    at_owner = lax.all_to_all(by_degree, "lat", split_axis=1, concat_axis=0, tiled=True)
    degree_local = inverse.shape[0]
    row_block = inverse.shape[1]
    full_rows = inverse.shape[2]
    matrices = inverse.reshape(degree_local, row_block, 2, full_rows // 2)
    return jnp.einsum(
        "tqfk,mtfck->tqcm",
        matrices,
        lax.all_gather(at_owner, "rad", axis=4, tiled=True),
        preferred_element_type=jnp.float32,
    )


def solution(mesh):
    in_specs = (
        P(None, None, "rad", None, None, "lat"),
        P("lat", None, None),
        P("lat", "rad", None),
        P(),
        P(),
        P(),
    )
    out_specs = P("lat", "rad", None, None)
    return jax.shard_map(
        on_device, mesh=mesh, in_specs=in_specs, out_specs=out_specs, check_vma=False
    )
```

profile of v0, /device:TPU:1, one launch (start us, length us, event | category | flops | bytes accessed | tf_op | source)
XLA Modules:
  0.0 196.2 jit_solution(13776918970840271404)
XLA Ops:
  6.5 0.0 copy-start
  6.5 0.8 compare_select_fusion.1
  7.3 0.7 compare_and_fusion.1
  8.0 7.4 %copy.17 = bf16[2,2,32,2,64,18]{2,5,3,1,0,4:T(8,128)(2,1)} copy(bf16[2,2,32,2,64,18]{4,3,5,2,1,0:T(2,128)(2,1)} %param.6) | data formatting | bytes 1179648 | tf_op args[0]
  15.4 4.5 %gather_fusion = bf16[64,2,2,32,2,18]{3,5,4,2,1,0:T(8,128)(2,1)} fusion(bf16[2,2,32,2,64,18]{2,5,3,1,0,4:T(8,128)(2,1)} %copy.17, s32[1024]{0:T(1024)S(1)} %pad_clamp_fusion), kind=kCustom, calls=%fused_computation | custom fusion | bytes 1179904 | tf_op jit(solution)/shard_map/jit(_take)/gather | solution.py:33
  19.9 2.2 %select_bitcast_fusion = bf16[2,2,32,2,64,18]{2,5,3,1,0,4:T(8,128)(2,1)S(1)} fusion(bf16[64,2,2,32,2,18]{3,5,4,2,1,0:T(8,128)(2,1)} %gather_fusion, pred[64]{0:T(512)(128)(4,1)S(1)} %compare_and_fusion.1), kind=kLoop, calls=%fused_computation.2 | loop fusion | flops 294912 | bytes 1179712 | tf_op jit(solution)/shard_map/jit(_take)/select_n | solution.py:33
  22.2 3.8 %copy.36 = bf16[2,2,32,2,64,18]{2,3,5,1,0,4:T(2,128)(2,1)} copy(bf16[2,2,32,2,64,18]{2,5,3,1,0,4:T(8,128)(2,1)S(1)} %select_bitcast_fusion) | data formatting | bytes 1179648 | tf_op jit(solution)/shard_map/jit(_take)/select_n | solution.py:33
  26.0 0.0 copy-start.2
  26.0 0.0 copy-start.3
  26.0 0.0 copy-start.1
  26.0 6.4 %reshape.148 = bf16[64,2,2304]{2,1,0:T(2,128)(2,1)} reshape(bf16[64,2,2,18,2,32]{5,4,3,2,1,0:T(2,128)(2,1)} %bitcast.59) | data formatting | bytes 1179648
  32.4 14.8 %all-to-all-start = ((bf16[64,2,2304]{2,1,0:T(2,128)(2,1)}), bf16[64,2,2304]{2,1,0:T(2,128)(2,1)S(1)}, u32[]{:S(2)}, u32[]{:S(2)}) async-start(bf16[64,2,2304]{2,1,0:T(2,128)(2,1)} %reshape.148), calls=%async_computation | async-start | bytes 1179648 | tf_op jit(solution)/shard_map/all_to_all | solution.py:34
  47.3 0.2 all-gather.2.cloned.1.call-start
  47.5 0.0 copy-done.2
  47.5 0.6 dynamic_slice.3
  50.0 0.0 copy-done.3
  50.0 0.6 dynamic-slice.2
  51.3 0.0 copy-done.1
  51.4 14.9 %all-to-all-done = bf16[64,2,2304]{2,1,0:T(2,128)(2,1)S(1)} async-done(((bf16[64,2,2304]{2,1,0:T(2,128)(2,1)}), bf16[64,2,2304]{2,1,0:T(2,128)(2,1)S(1)}, u32[]{:S(2)}, u32[]{:S(2)}) %all-to-all-start) | async-done | bytes 589856 | tf_op jit(solution)/shard_map/all_to_all | solution.py:34
  66.3 2.4 %reshape.149 = bf16[64,2,2,18,2,32]{5,4,3,2,1,0:T(2,128)(2,1)} reshape(bf16[64,2,2304]{2,1,0:T(2,128)(2,1)S(1)} %all-to-all-done) | data formatting | bytes 1179648
  68.6 10.1 %copy.19 = bf16[2,2,32,2,64,18]{5,4,2,3,1,0:T(8,128)(2,1)} copy(bf16[2,2,32,2,64,18]{2,3,5,1,0,4:T(2,128)(2,1)} %bitcast.58) | data formatting | bytes 1179648 | tf_op jit(solution)/shard_map/all_to_all | solution.py:34
  78.7 7.0 %all_to_all.9 = bf16[2,2,32,2,1,1152]{5,2,3,1,0,4:T(8,128)(2,1)S(1)} reshape(bf16[2,2,32,2,64,18]{5,4,2,3,1,0:T(8,128)(2,1)} %copy.19) | data formatting | bytes 1179648 | tf_op jit(solution)/shard_map/all_to_all | solution.py:34
  85.7 0.0 copy-done
  85.7 0.9 fusion
  86.6 1.6 fusion.13
  88.2 2.2 %copy.20 = bf16[1024,2,2,32]{3,2,1,0:T(2,128)(2,1)S(1)} copy(bf16[1024,2,2,32]{0,3,2,1:T(8,128)(2,1)} %fusion.13) | data formatting | bytes 524288 | tf_op jit(solution)/shard_map/convert_element_type | solution.py:24
  90.4 8.5 %gather_fusion.1 = bf16[1024,2,2,32]{3,2,1,0:T(2,128)(2,1)} fusion(bf16[1024,2,2,32]{3,2,1,0:T(2,128)(2,1)S(1)} %copy.20, s32[1024]{0:T(1024)S(1)} %fusion.33), kind=kCustom, calls=%fused_computation.1 | custom fusion | bytes 528384 | tf_op jit(solution)/shard_map/jit(_take)/gather | solution.py:36
  99.0 5.3 %fusion.34 = bf16[1024,1,2,2,32]{4,3,2,1,0:T(2,128)(2,1)S(1)} fusion(bf16[1024,2,2,32]{3,2,1,0:T(2,128)(2,1)} %gather_fusion.1, pred[1024]{0:T(1024)(128)(4,1)S(1)} %compare_and_fusion), kind=kLoop, calls=%fused_computation.41 | loop fusion | flops 131072 | bytes 525312
  104.3 1.7 reshape.150
  106.0 18.9 %all_to_all.24 = bf16[64,2,1024]{2,1,0:T(2,128)(2,1)} all-to-all(bf16[64,2,1024]{2,1,0:T(2,128)(2,1)} %reshape.150), channel_id=1, replica_groups=mesh['lat'=64,'rad'=8] {'lat'}, dimensions={0} | all-to-all | bytes 524288 | tf_op jit(solution)/shard_map/all_to_all | solution.py:37
  124.9 3.0 %reshape.151 = bf16[1024,1,2,2,32]{4,3,2,1,0:T(2,128)(2,1)S(1)} reshape(bf16[64,2,1024]{2,1,0:T(2,128)(2,1)} %all_to_all.24) | data formatting | bytes 524288
  128.0 2.2 %copy.23 = bf16[64,16,2,2,32]{0,4,2,3,1:T(8,128)(2,1)} copy(bf16[64,16,2,2,32]{4,3,2,1,0:T(2,128)(2,1)S(1)} %bitcast.60) | data formatting | bytes 524288 | tf_op jit(solution)/shard_map/all_to_all | solution.py:37
  130.1 0.0 all-gather.2.cloned.1.call-update
  130.2 1.3 reshape.96
  131.5 51.1 %all-gather.2.cloned.1.call-done = bf16[64,16,2,2,256]{0,4,2,3,1:T(8,128)(2,1)} async-done(((bf16[64,16,2,2,32]{0,4,2,3,1:T(8,128)(2,1)}), bf16[64,16,2,2,256]{0,4,2,3,1:T(8,128)(2,1)}) %all-gather.2.cloned.1.call-update) | async-done | bytes 2097168 | tf_op jit(solution)/shard_map/all_gather | solution.py:45
  182.7 4.4 %convolution_bitcast_fusion = f32[16,64,2,64]{1,3,2,0:T(8,128)} fusion(bf16[64,16,2,2,256]{0,4,2,3,1:T(8,128)(2,1)} %all-gather.2.cloned.1.call-done, bf16[16,64,2,256,1]{3,2,1,0,4:T(2,128)(2,1)S(1)} %bitcast.61), kind=kOutput, calls=%fused_computation.8 | convolution fusion | flops 134217728 | bytes 3670016 | tf_op jit(solution)/shard_map/tqfk,mtfck->tqcm/dot_general | solution.py:42
  187.1 2.2 %copy.25 = f32[16,64,2,64]{3,2,1,0:T(2,128)} copy(f32[16,64,2,64]{1,3,2,0:T(8,128)} %convolution_bitcast_fusion) | data formatting | bytes 1048576 | tf_op jit(solution)/shard_map/tqfk,mtfck->tqcm/transpose | solution.py:42
  (4 shorter events, 0.0 us)
Async XLA Ops:
  6.5 79.2 %copy-start = (bf16[1,1024,1152]{2,1,0:T(8,128)(2,1)S(1)}, bf16[1,1024,1152]{2,1,0:T(8,128)(2,1)}, u32[]{:S(2)}) copy-start(bf16[1,1024,1152]{2,1,0:T(8,128)(2,1)} %param.7) | copy-start | bytes 7077892
  26.0 21.5 %copy-start.2 = (s32[64]{0:T(128)S(1)}, s32[64]{0:T(128)}, u32[]{:S(2)}) copy-start(s32[64]{0:T(128)} %param.9) | copy-start | bytes 772
  26.0 24.0 %copy-start.3 = (s32[64]{0:T(128)S(1)}, s32[64]{0:T(128)}, u32[]{:S(2)}) copy-start(s32[64]{0:T(128)} %param.11) | copy-start | bytes 772
  26.0 25.3 %copy-start.1 = (s32[1024]{0:T(1024)S(1)}, s32[1024]{0:T(1024)}, u32[]{:S(2)}) copy-start(s32[1024]{0:T(1024)} %param.10) | copy-start | bytes 12292
  32.4 33.8 %all-to-all-start = ((bf16[64,2,2304]{2,1,0:T(2,128)(2,1)}), bf16[64,2,2304]{2,1,0:T(2,128)(2,1)S(1)}, u32[]{:S(2)}, u32[]{:S(2)}) async-start(bf16[64,2,2304]{2,1,0:T(2,128)(2,1)} %reshape.148), calls=%async_computation | async-start | bytes 1179648 | tf_op jit(solution)/shard_map/all_to_all | solution.py:34
  47.3 135.4 %all-gather.2.cloned.1.call-start = ((), (), s32[]{:S(2)}) async-start(), calls=%async_computation.2 | async-start | bytes 4718592 | tf_op jit(solution)/shard_map/all_gather | solution.py:45
Sparse Core Ops, SparseCore 0:
  130.3 52.3 all-gather.1
where the time goes:
time: 197 us; the launch traced here: 196 us
  waiting for transfers between devices  66.1 us (34%)
  local copies, waits for them, and re-layouts  64.1 us (33%)
  blocking collectives  18.9 us (10%)
  between operations  16.1 us (8%)
  starting transfers between devices  15 us (8%)
  other arithmetic  9.07 us (5%)
  matrix products  6.89 us (3%)
    all_gather x1, waiting for transfers between devices, on_device(): lax.all_gather(at_owner, 'rad', axis=4, tiled=True)  51.1 us
    unnamed x13, local copies, waits for them, and re-layouts  20.9 us
    all_to_all x1, blocking collectives, on_device(): lax.all_to_all(by_degree, 'lat', split_axis=1, concat_axis=0, tiled=True)  18.9 us
    all_to_all x2, local copies, waits for them, and re-layouts, on_device(): lax.all_to_all(picked, 'lat', split_axis=4, concat_axis=5, tiled=True)  17.1 us
    all_to_all x1, waiting for transfers between devices, on_device(): lax.all_to_all(picked, 'lat', split_axis=4, concat_axis=5, tiled=True)  14.9 us
    all_to_all x1, starting transfers between devices, on_device(): lax.all_to_all(picked, 'lat', split_axis=4, concat_axis=5, tiled=True)  14.8 us
    gather x1, local copies, waits for them, and re-layouts, on_device(): by_degree = jnp.take(coefficients, degree_of_slot, axis=1)  8.52 us
    unnamed x1, other arithmetic  5.34 us
  transfers between devices with their start and end apart: 2, of which 2 were waited for; matrix products, arithmetic and copies ran while one was open for 1% of the time, Pallas kernels for 0%

commit v1 on v0

v1 whole, which is shorter than its diff:
```python
import functools

import jax
import jax.numpy as jnp
from jax import lax
from jax.experimental import pallas as pl
from jax.experimental.pallas import tpu as pltpu
from jax.sharding import PartitionSpec as P

BF16 = jnp.bfloat16
F32 = jnp.float32
MESH = pl.DeviceIdType.MESH
LANES = 128
CHUNKS = 4


def iota(shape, dim):
    return lax.broadcasted_iota(jnp.int32, shape, dim)


def column(row):
    return jnp.transpose(jnp.broadcast_to(row, (LANES, row.shape[1])))


def dot_nt(a, b):
    return lax.dot_general(a, b, (((1,), (1,)), ((), ())), preferred_element_type=F32)


def kernel(
    dims,
    order_ref, degree_ref, count_ref, rows_hbm, table_hbm, inverse_hbm,
    out_ref,
    rows, table, inverse, north, south, send_even, send_odd, recv_even, recv_odd,
    pick, column_degree, table_live, send_c, recv_c, wide, gathered, spread, total,
    rows_sem, table_sem, inverse_sem, send1, recv1, send2, recv2,
    send_up, send_down, recv_up, recv_down,
):
    n_lat, n_rad, n_l, n_deg, n_t = dims
    me = lax.axis_index("lat")
    y = lax.axis_index("rad")
    up, down = lax.rem(y + 1, n_rad), lax.rem(y + n_rad - 1, n_rad)
    group = min(8, n_lat)
    planes = n_lat // group

    def load_rows(l):
        return pltpu.make_async_copy(rows_hbm.at[:, l], rows.at[l], rows_sem.at[l])

    for l in range(n_l):
        load_rows(l).start()
    load_table = pltpu.make_async_copy(table_hbm, table, table_sem)
    load_table.start()
    load_inverse = pltpu.make_async_copy(inverse_hbm, inverse, inverse_sem)
    load_inverse.start()

    barrier = pltpu.get_barrier_semaphore()

    def greet(k, carry):
        pl.semaphore_signal(
            barrier, inc=1, device_id={"lat": lax.rem(me + k, n_lat)}, device_id_type=MESH
        )
        return carry

    lax.fori_loop(1, n_lat, greet, 0)
    for other in (up, down):
        pl.semaphore_signal(barrier, inc=1, device_id={"rad": other}, device_id_type=MESH)

    order = order_ref[...].astype(F32)
    order_column = column(order)[:, :n_lat]
    order_pick = jnp.where(
        order_column == iota((n_lat, n_lat), 1).astype(F32), 1.0, 0.0
    ).astype(BF16)
    for l in range(n_l):
        load_rows(l).wait()
        picked = dot_nt(order_pick, rows.at[l].reshape(2 * LANES, n_lat)[...])
        north[pl.ds(l, n_lat, stride=n_l), :] = picked[:, :LANES]
        south[pl.ds(l, n_lat, stride=n_l), :] = picked[:, LANES:]

    source, target = iota((2 * LANES, 2 * LANES), 0), iota((2 * LANES, 2 * LANES), 1)
    fold = jnp.where(
        source // 2 == target % LANES,
        jnp.where((source % 2 == 1) & (target >= LANES), -1.0, 1.0),
        0.0,
    ).astype(BF16)

    pl.semaphore_wait(barrier, n_lat + 1)

    def fold_and_send(k, carry):
        far = lax.select(lax.rem(k, 2) == 0, k // 2, lax.rem(planes - k // 2, planes))
        plane = lax.rem(me // group + far, planes)
        at = pl.ds(pl.multiple_of(plane * (group * n_l), 16), group * n_l)
        both = jnp.concatenate([north[at, :], south[at, :]], axis=1).astype(BF16)
        folded = jnp.dot(both, fold, preferred_element_type=F32).astype(BF16)
        send_even.reshape(n_lat * n_l, LANES)[at, :] = folded[:, :LANES]
        send_odd.reshape(n_lat * n_l, LANES)[at, :] = folded[:, LANES:]

        def send(i, c):
            peer = plane * group + lax.rem(me + i, group)

            @pl.when(peer != me)
            def _():
                for p, (src, dst) in enumerate(((send_even, recv_even), (send_odd, recv_odd))):
                    pltpu.make_async_remote_copy(
                        src_ref=src.at[peer], dst_ref=dst.at[me],
                        send_sem=send1.at[p], recv_sem=recv1.at[p],
                        device_id={"lat": peer}, device_id_type=MESH,
                    ).start()

            @pl.when(peer == me)
            def _():
                for p, (src, dst) in enumerate(((send_even, recv_even), (send_odd, recv_odd))):
                    pltpu.make_async_copy(src.at[me], dst.at[me], recv1.at[p]).start()

            return c

        return lax.fori_loop(0, group, send, carry)

    lax.fori_loop(1, planes + 1, fold_and_send, 0)

    mine = jnp.sum(jnp.where(iota((1, n_lat), 1) == me, order, 0.0), axis=1, keepdims=True)
    count = jnp.sum(
        jnp.where(iota((1, n_lat), 1).astype(F32) == mine, count_ref[...].astype(F32), 0.0),
        axis=1, keepdims=True,
    )
    first = n_deg - count
    blocks, block = degree_ref.shape

    def pick_rows(b, carry):
        at = pl.ds(pl.multiple_of(b * block, block), block)
        held = column(degree_ref[pl.ds(b, 1), :].astype(F32))
        column_degree[at, :] = held
        for j in range(blocks):
            lane = (iota((block, block), 1) + j * block).astype(F32)
            cell = held[:, :block]
            pick[at, j * block:(j + 1) * block] = jnp.where(
                (cell == lane) & (cell >= first), 1.0, 0.0
            ).astype(BF16)
        return carry

    lax.fori_loop(0, blocks, pick_rows, 0)
    load_table.wait()
    rows_at_once = min(256, n_deg)

    def order_rows(b, carry):
        at = pl.ds(pl.multiple_of(b * rows_at_once, rows_at_once), rows_at_once)
        table_live[at, :] = jnp.dot(
            pick[at, :], table[...], preferred_element_type=F32
        ).astype(BF16)
        return carry

    lax.fori_loop(0, n_deg // rows_at_once, order_rows, 0)

    pltpu.make_async_copy(recv_even, recv_even, recv1.at[0]).wait()
    pltpu.make_async_copy(recv_odd, recv_odd, recv1.at[1]).wait()

    parts = n_deg // rows_at_once
    slots_at_once = rows_at_once // n_t

    def analyse_and_send(k, carry):
        part = lax.rem(me // slots_at_once + k, parts)
        at = pl.ds(pl.multiple_of(part * rows_at_once, rows_at_once), rows_at_once)
        both = jnp.concatenate(
            [
                recv_even.reshape(n_lat * n_l, LANES)[...],
                recv_odd.reshape(n_lat * n_l, LANES)[...],
            ],
            axis=1,
        )
        product = jnp.dot(table_live[at, :], both, preferred_element_type=F32)
        parity = (column_degree[at, :] - first).astype(jnp.int32) & 1
        send_c[at, :] = jnp.where(
            parity == 0, product[:, :LANES], product[:, LANES:]
        ).astype(BF16)

        def send(i, c):
            peer = part * slots_at_once + lax.rem(me + i, slots_at_once)
            src = send_c.at[pl.ds(pl.multiple_of(peer * n_t, n_t), n_t), :]
            dst = recv_c.at[pl.ds(pl.multiple_of(me * n_t, n_t), n_t), :]

            @pl.when(peer != me)
            def _():
                pltpu.make_async_remote_copy(
                    src_ref=src, dst_ref=dst, send_sem=send2, recv_sem=recv2,
                    device_id={"lat": peer}, device_id_type=MESH,
                ).start()

            @pl.when(peer == me)
            def _():
                pltpu.make_async_copy(src, dst, recv2).start()

            return c

        return lax.fori_loop(0, slots_at_once, send, carry)

    lax.fori_loop(0, parts, analyse_and_send, 0)

    load_inverse.wait()
    flat_inverse = inverse.reshape(inverse.shape[0] * inverse.shape[1], inverse.shape[2])
    n_q, full = inverse.shape[1], inverse.shape[2]
    radii = full // 2 // n_rad

    def spread_columns(o, carry):
        row, col = iota((full, 2 * LANES), 0), iota((full, 2 * LANES), 1)
        lane = col % LANES
        wanted = (lane // (2 * radii)) * (full // 2) + o * radii + lane % radii
        part = (lane // radii) % 2
        place = jnp.where((row == wanted) & (part == col // LANES), 1.0, 0.0).astype(BF16)
        placed = jnp.dot(flat_inverse[...], place, preferred_element_type=F32).astype(BF16)
        for t in range(n_t):
            for c in range(2):
                spread[o, t, c * n_q:(c + 1) * n_q, :] = placed[
                    t * n_q:(t + 1) * n_q, c * LANES:(c + 1) * LANES
                ]
        return carry

    lax.fori_loop(0, n_rad, spread_columns, 0)

    pltpu.make_async_copy(recv_c, recv_c, recv2).wait()
    wide[...] = recv_c[...].astype(F32)
    for t in range(n_t):
        gathered[y, t] = wide[pl.ds(t, n_lat, stride=n_t), :].astype(BF16)

    per = n_t // CHUNKS
    half = n_rad // 2

    def pass_on(upwards, origin, step, c):
        sems = (send_up, recv_up) if upwards else (send_down, recv_down)
        block_ref = gathered.at[origin, pl.ds(c * per, per)]
        return pltpu.make_async_remote_copy(
            src_ref=block_ref, dst_ref=block_ref,
            send_sem=sems[0].at[step], recv_sem=sems[1].at[step, c],
            device_id={"rad": up if upwards else down}, device_id_type=MESH,
        )

    def send_own(c, carry):
        pass_on(True, y, 0, c).start()
        pass_on(False, y, 0, c).start()
        return carry

    lax.fori_loop(0, CHUNKS, send_own, 0)

    def add(origins, c, init):
        for i in range(per):
            t = c * per + i
            a = [spread[o, t] for o in origins]
            b = [gathered[o, t] for o in origins]
            a = a[0] if len(a) == 1 else jnp.concatenate(a, axis=1)
            b = b[0] if len(b) == 1 else jnp.concatenate(b, axis=1)
            term = dot_nt(a, b)
            if init:
                total[t] = term
            else:
                total[t] += term

    def add_own(c, carry):
        add([y], c, True)
        return carry

    lax.fori_loop(0, CHUNKS, add_own, 0)

    for step in range(1, half):
        below, above = lax.rem(y + n_rad - step, n_rad), lax.rem(y + step, n_rad)

        def relay(c, carry):
            pass_on(True, below, step - 1, c).wait_recv()
            if step < half - 1:
                pass_on(True, below, step, c).start()
            else:
                @pl.when(c < CHUNKS // 2)
                def _():
                    pass_on(True, below, step, c).start()
            pass_on(False, above, step - 1, c).wait_recv()
            if step < half - 1:
                pass_on(False, above, step, c).start()
            else:
                @pl.when(c >= CHUNKS // 2)
                def _():
                    pass_on(False, above, step, c).start()
            add([below, above], c, False)
            return carry

        lax.fori_loop(0, CHUNKS, relay, 0)

    opposite = lax.rem(y + half, n_rad)
    for c in range(CHUNKS // 2):
        for upwards in (True, False):
            at = c if upwards else c + CHUNKS // 2
            pass_on(upwards, opposite, half - 1, at).wait_recv()
            add([opposite], at, False)

    flat_out = out_ref.reshape(n_t * n_q * 2, n_lat)
    for t in range(n_t):
        for c in range(2):
            flat_out[pl.ds(t * n_q * 2 + c, n_q, stride=2), :] = total[t, c * n_q:(c + 1) * n_q, :]

    others = pl.ds(0, n_lat - 1)
    pltpu.make_async_copy(send_even.at[others], send_even.at[others], send1.at[0]).wait()
    pltpu.make_async_copy(send_odd.at[others], send_odd.at[others], send1.at[1]).wait()
    most = send_c.at[pl.ds(0, (n_lat - 1) * n_t), :]
    pltpu.make_async_copy(most, most, send2).wait()
    for sem in (send_up, send_down):
        for step in range(half):
            sent = gathered.at[0, pl.ds(0, n_t if step < half - 1 else n_t // 2)]
            pltpu.make_async_copy(sent, sent, sem.at[step]).wait()


def on_device(n_lat, n_rad, fourier, legendre, inverse, order_of_slot, degree_of_slot, degree_count):
    f, c, r, h, m, n_l = fourier.shape
    n_deg, n_h = legendre.shape[1:]
    n_t, n_q, full = inverse.shape
    half = n_rad // 2
    rows = jnp.transpose(fourier, (0, 1, 2, 5, 3, 4)).reshape(f * c * r, n_l, h, m)
    block = min(LANES, n_deg)
    any_space = pl.BlockSpec(memory_space=pl.ANY)
    in_vmem = pl.BlockSpec(memory_space=pltpu.VMEM)
    dma = pltpu.SemaphoreType.DMA
    pairs = (n_lat, n_l // 2, 2, LANES)
    return pl.pallas_call(
        functools.partial(kernel, (n_lat, n_rad, n_l, n_deg, n_t)),
        out_shape=jax.ShapeDtypeStruct((n_t, n_q, c, n_lat), F32),
        in_specs=[in_vmem] * 3 + [any_space] * 3,
        out_specs=in_vmem,
        scratch_shapes=[
            pltpu.VMEM((n_l, f * c * r, h, m), BF16),
            pltpu.VMEM((n_deg, n_h), BF16),
            pltpu.VMEM((n_t, n_q, full), BF16),
            pltpu.VMEM((n_lat * n_l, LANES), F32),
            pltpu.VMEM((n_lat * n_l, LANES), F32),
            pltpu.VMEM(pairs, BF16),
            pltpu.VMEM(pairs, BF16),
            pltpu.VMEM(pairs, BF16),
            pltpu.VMEM(pairs, BF16),
            pltpu.VMEM((n_deg, n_deg), BF16),
            pltpu.VMEM((n_deg, LANES), F32),
            pltpu.VMEM((n_deg, n_h), BF16),
            pltpu.VMEM((n_deg, LANES), BF16),
            pltpu.VMEM((n_lat * n_t, LANES), BF16),
            pltpu.VMEM((n_lat * n_t, LANES), F32),
            pltpu.VMEM((n_rad, n_t, n_lat, LANES), BF16),
            pltpu.VMEM((n_rad, n_t, c * n_q, LANES), BF16),
            pltpu.VMEM((n_t, c * n_q, n_lat), F32),
            dma((n_l,)), dma, dma,
            dma((2,)), dma((2,)), dma, dma,
            dma((half,)), dma((half,)), dma((half, CHUNKS)), dma((half, CHUNKS)),
        ],
        compiler_params=pltpu.CompilerParams(
            collective_id=0, has_side_effects=True, vmem_limit_bytes=56 << 20
        ),
    )(
        order_of_slot.reshape(1, n_lat),
        degree_of_slot.reshape(n_deg // block, block),
        degree_count.reshape(1, n_lat),
        rows,
        legendre.reshape(n_deg, n_h),
        inverse,
    )


def solution(mesh):
    in_specs = (
        P(None, None, "rad", None, None, "lat"),
        P("lat", None, None),
        P("lat", "rad", None),
        P(),
        P(),
        P(),
    )
    out_specs = P("lat", "rad", None, None)
    body = functools.partial(on_device, mesh.shape["lat"], mesh.shape["rad"])
    return jax.shard_map(
        body, mesh=mesh, in_specs=in_specs, out_specs=out_specs, check_vma=False
    )
```

time: 197 us -> 71.9 us (0.36)
  Pallas kernels: 0 us -> 69.4 us
  waiting for transfers between devices: 66.1 us -> 0 us
  local copies, waits for them, and re-layouts: 64.1 us -> 2.3 us
  blocking collectives: 18.9 us -> 0 us
  between operations: 16.1 us -> 0.01 us
  starting transfers between devices: 15 us -> 0 us
  other arithmetic: 9.07 us -> 0 us
  matrix products: 6.89 us -> 0 us
    pallas_call x0 -> x1, Pallas kernels: none -> 69.4 us  [on_device(): pl.pallas_call(functools.partial(kernel, (n_lat, n_rad, n_l, n_deg, n_t))...]
    all_gather x1 -> x0, waiting for transfers between devices: 51.1 us -> none  [on_device(): lax.all_gather(at_owner, 'rad', axis=4, tiled=True)]
    all_to_all x3 -> x0, local copies, waits for them, and re-layouts: 19.2 us -> none  [the longest x2 17.1 us: on_device(): lax.all_to_all(picked, 'lat', split_axis=4, concat_axis=5, tiled=True)]
    all_to_all x1 -> x0, blocking collectives: 18.9 us -> none  [on_device(): lax.all_to_all(by_degree, 'lat', split_axis=1, concat_axis=0, tiled=True)]
    unnamed x13 -> x1, local copies, waits for them, and re-layouts: 20.9 us -> 2.3 us
    all_to_all x1 -> x0, waiting for transfers between devices: 14.9 us -> none  [on_device(): lax.all_to_all(picked, 'lat', split_axis=4, concat_axis=5, tiled=True)]
    all_to_all x1 -> x0, starting transfers between devices: 14.8 us -> none  [on_device(): lax.all_to_all(picked, 'lat', split_axis=4, concat_axis=5, tiled=True)]
    gather x3 -> x0, local copies, waits for them, and re-layouts: 13.7 us -> none  [the longest x1 8.52 us: on_device(): by_degree = jnp.take(coefficients, degree_of_slot, axis=1)]
  transfers between devices with their start and end apart: 2 -> 0, of which waited for: 2 -> 0; matrix products, arithmetic and copies ran while one was open for 1% -> 0% of each run, Pallas kernels for 0% -> 0%
where the time goes in v1:
time: 71.9 us; the launch traced here: 71.7 us
  Pallas kernels  69.4 us (97%)
  local copies, waits for them, and re-layouts  2.3 us (3%)
    pallas_call x1, Pallas kernels, on_device(): pl.pallas_call(functools.partial(kernel, (n_lat, n_rad, n_l, n_deg, n_t))...  69.4 us
    unnamed x1, local copies, waits for them, and re-layouts  2.3 us

profile of v1, /device:TPU:1, one launch (start us, length us, event | category | flops | bytes accessed | tf_op | source)
XLA Modules:
  0.0 71.7 jit_solution(4053241655473414966)
XLA Ops:
  0.0 69.4 %shard_map.64 = f32[16,64,2,64]{3,2,1,0:T(2,128)} custom-call(s32[1,64]{1,0:T(1,128)} %bitcast.10, s32[8,128]{1,0:T(8,128)} %bitcast.9, s32[1,64]{1,0:T(1,128)} %bitcast.11, bf16[128,18,2,64]{3,2,1,0:T(2,128)(2,1)} %bitcast.8, bf16[1024,1152]{1,0:T(8,128)(2,1)} %bitcast.7, bf16[16,64,512]{2,1,0:T(8,128)(2,1)} %inverse_hbm.1), custom_call_target="tpu_custom_call" | custom-call | tf_op jit(solution)/shard_map/pallas_call | solution.py:317
  69.4 2.3 %copy.8 = f32[16,64,2,64]{3,2,1,0:T(2,128)} copy(f32[16,64,2,64]{3,2,1,0:T(2,128)} %shard_map.64) | data formatting | bytes 1048576

commit v2 on v1

v2 whole, which is shorter than its diff:
```python
import functools

import jax
import jax.numpy as jnp
from jax import lax
from jax.experimental import pallas as pl
from jax.experimental.pallas import tpu as pltpu
from jax.sharding import PartitionSpec as P

BF16 = jnp.bfloat16
F32 = jnp.float32
MESH = pl.DeviceIdType.MESH
LANES = 128


def iota(shape, dim):
    return lax.broadcasted_iota(jnp.int32, shape, dim)


def column(row):
    return jnp.transpose(jnp.broadcast_to(row, (LANES, row.shape[1])))


def dot_nt(a, b):
    return lax.dot_general(a, b, (((1,), (1,)), ((), ())), preferred_element_type=F32)


def kernel(
    dims,
    order_ref, degree_ref, count_ref, rows_hbm, table_hbm, inverse_hbm,
    out_ref,
    rows, table, north, south, send_even, send_odd, recv_even, recv_odd,
    natural_degree, pick, column_degree, table_live, send_c, recv_c, wide,
    bring_c, got_c, matrices, right_side, send_o, recv_o,
    rows_sem, table_sem, send0, recv0, send1, recv1, send2, recv2, send3, recv3, send4, recv4,
):
    n_lat, n_rad, n_l, n_deg, n_t = dims
    own = n_t // n_rad
    n_q, full = matrices.shape[2], matrices.shape[3]
    radii = full // 2 // n_rad
    me = lax.axis_index("lat")
    y = lax.axis_index("rad")
    group = min(8, n_lat)
    planes = n_lat // group

    def load_rows(l):
        return pltpu.make_async_copy(rows_hbm.at[:, l], rows.at[l], rows_sem.at[l])

    for l in range(n_l):
        load_rows(l).start()
    load_table = pltpu.make_async_copy(table_hbm, table, table_sem)
    load_table.start()

    barrier = pltpu.get_barrier_semaphore()

    def greet_lat(k, carry):
        pl.semaphore_signal(
            barrier, inc=1, device_id={"lat": lax.rem(me + k, n_lat)}, device_id_type=MESH
        )
        return carry

    def greet_rad(k, carry):
        pl.semaphore_signal(
            barrier, inc=1, device_id={"rad": lax.rem(y + k, n_rad)}, device_id_type=MESH
        )
        return carry

    lax.fori_loop(1, n_lat, greet_lat, 0)
    lax.fori_loop(1, n_rad, greet_rad, 0)

    order = order_ref[...].astype(F32)
    order_column = column(order)[:, :n_lat]
    order_pick = jnp.where(
        order_column == iota((n_lat, n_lat), 1).astype(F32), 1.0, 0.0
    ).astype(BF16)
    for l in range(n_l):
        load_rows(l).wait()
        picked = dot_nt(order_pick, rows.at[l].reshape(2 * LANES, n_lat)[...])
        north[pl.ds(l, n_lat, stride=n_l), :] = picked[:, :LANES]
        south[pl.ds(l, n_lat, stride=n_l), :] = picked[:, LANES:]

    source, target = iota((2 * LANES, 2 * LANES), 0), iota((2 * LANES, 2 * LANES), 1)
    fold = jnp.where(
        source // 2 == target % LANES,
        jnp.where((source % 2 == 1) & (target >= LANES), -1.0, 1.0),
        0.0,
    ).astype(BF16)

    pl.semaphore_wait(barrier, n_lat + n_rad - 2)

    def send_matrices(k, carry):
        peer = lax.rem(y + k, n_rad)
        pltpu.make_async_remote_copy(
            src_ref=inverse_hbm.at[pl.ds(peer * own, own)], dst_ref=matrices.at[:, y],
            send_sem=send0, recv_sem=recv0,
            device_id={"rad": peer}, device_id_type=MESH,
        ).start()
        return carry

    lax.fori_loop(1, n_rad, send_matrices, 0)
    pltpu.make_async_copy(inverse_hbm.at[pl.ds(y * own, own)], matrices.at[:, y], recv0).start()

    def fold_and_send(k, carry):
        far = lax.select(lax.rem(k, 2) == 0, k // 2, lax.rem(planes - k // 2, planes))
        plane = lax.rem(me // group + far, planes)
        at = pl.ds(pl.multiple_of(plane * (group * n_l), 16), group * n_l)
        both = jnp.concatenate([north[at, :], south[at, :]], axis=1).astype(BF16)
        folded = jnp.dot(both, fold, preferred_element_type=F32).astype(BF16)
        send_even.reshape(n_lat * n_l, LANES)[at, :] = folded[:, :LANES]
        send_odd.reshape(n_lat * n_l, LANES)[at, :] = folded[:, LANES:]

        def send(i, c):
            peer = plane * group + lax.rem(me + i, group)

            @pl.when(peer != me)
            def _():
                for p, (src, dst) in enumerate(((send_even, recv_even), (send_odd, recv_odd))):
                    pltpu.make_async_remote_copy(
                        src_ref=src.at[peer], dst_ref=dst.at[me],
                        send_sem=send1.at[p], recv_sem=recv1.at[p],
                        device_id={"lat": peer}, device_id_type=MESH,
                    ).start()

            @pl.when(peer == me)
            def _():
                for p, (src, dst) in enumerate(((send_even, recv_even), (send_odd, recv_odd))):
                    pltpu.make_async_copy(src.at[me], dst.at[me], recv1.at[p]).start()

            return c

        return lax.fori_loop(0, group, send, carry)

    lax.fori_loop(1, planes + 1, fold_and_send, 0)

    mine = jnp.sum(jnp.where(iota((1, n_lat), 1) == me, order, 0.0), axis=1, keepdims=True)
    count = jnp.sum(
        jnp.where(iota((1, n_lat), 1).astype(F32) == mine, count_ref[...].astype(F32), 0.0),
        axis=1, keepdims=True,
    )
    first = n_deg - count
    blocks, block = degree_ref.shape

    def to_column(b, carry):
        at = pl.ds(pl.multiple_of(b * block, block), block)
        natural_degree[at, :] = column(degree_ref[pl.ds(b, 1), :].astype(F32))
        return carry

    lax.fori_loop(0, blocks, to_column, 0)
    step = n_deg // own // blocks

    for h in range(own):
        def pick_rows(b, carry):
            held = natural_degree[pl.ds(b * (step * own) + h, step, stride=own), :]
            at = pl.ds(pl.multiple_of(b * step + h * (n_deg // own), step), step)
            column_degree[at, :] = held
            for j in range(blocks):
                lane = (iota((step, block), 1) + j * block).astype(F32)
                cell = held[:, :block]
                pick[at, j * block:(j + 1) * block] = jnp.where(
                    (cell == lane) & (cell >= first), 1.0, 0.0
                ).astype(BF16)
            return carry

        lax.fori_loop(0, blocks, pick_rows, 0)

    load_table.wait()
    rows_at_once = min(256, n_deg // own)

    def order_rows(b, carry):
        at = pl.ds(pl.multiple_of(b * rows_at_once, rows_at_once), rows_at_once)
        table_live[at, :] = jnp.dot(
            pick[at, :], table[...], preferred_element_type=F32
        ).astype(BF16)
        return carry

    lax.fori_loop(0, n_deg // rows_at_once, order_rows, 0)

    pltpu.make_async_copy(recv_even, recv_even, recv1.at[0]).wait()
    pltpu.make_async_copy(recv_odd, recv_odd, recv1.at[1]).wait()

    parts = n_deg // own // rows_at_once
    peers = rows_at_once // n_rad

    for h in range(own):
        def analyse_and_send(k, carry):
            part = lax.rem(me // peers + k, parts)
            begin = pl.multiple_of(part * rows_at_once, rows_at_once)
            at = pl.ds(begin + h * (n_deg // own), rows_at_once)
            both = jnp.concatenate(
                [
                    recv_even.reshape(n_lat * n_l, LANES)[...],
                    recv_odd.reshape(n_lat * n_l, LANES)[...],
                ],
                axis=1,
            )
            product = jnp.dot(table_live[at, :], both, preferred_element_type=F32)
            parity = (column_degree[at, :] - first).astype(jnp.int32) & 1
            send_c.at[h].reshape(n_lat * n_rad, LANES)[pl.ds(begin, rows_at_once), :] = jnp.where(
                parity == 0, product[:, :LANES], product[:, LANES:]
            ).astype(BF16)

            def send(i, c):
                peer = part * peers + lax.rem(me + i, peers)
                src, dst = send_c.at[h, peer], recv_c.at[h, me]

                @pl.when(peer != me)
                def _():
                    pltpu.make_async_remote_copy(
                        src_ref=src, dst_ref=dst, send_sem=send2.at[h], recv_sem=recv2.at[h],
                        device_id={"lat": peer}, device_id_type=MESH,
                    ).start()

                @pl.when(peer == me)
                def _():
                    pltpu.make_async_copy(src, dst, recv2.at[h]).start()

                return c

            return lax.fori_loop(0, peers, send, carry)

        lax.fori_loop(0, parts, analyse_and_send, 0)

    for h in range(own):
        pltpu.make_async_copy(recv_c.at[h], recv_c.at[h], recv2.at[h]).wait()
        wide[h] = recv_c.at[h].reshape(n_lat * n_rad, LANES)[...].astype(F32)

        def bring(k, carry):
            peer = lax.rem(y + k, n_rad)
            bring_c[h, peer] = wide[h, pl.ds(peer, n_lat, stride=n_rad), :].astype(BF16)
            pltpu.make_async_remote_copy(
                src_ref=bring_c.at[h, peer], dst_ref=got_c.at[h, y],
                send_sem=send3.at[h], recv_sem=recv3.at[h],
                device_id={"rad": peer}, device_id_type=MESH,
            ).start()
            return carry

        lax.fori_loop(1, n_rad, bring, 0)
        got_c[h, y] = wide[h, pl.ds(y, n_lat, stride=n_rad), :].astype(BF16)

    pltpu.make_async_copy(matrices, matrices, recv0).wait()
    others = pl.ds(0, n_rad - 1)
    for h in range(own):
        pltpu.make_async_copy(got_c.at[h, others], got_c.at[h, others], recv3.at[h]).wait()
        for o in range(n_rad):
            turned = jnp.transpose(got_c[h, o].astype(F32))
            for f in range(2):
                pair = [turned[(2 * f + c) * radii:(2 * f + c + 1) * radii, :] for c in range(2)]
                right_side[h, f * (full // 2) + o * radii:f * (full // 2) + (o + 1) * radii, :] = (
                    jnp.concatenate(pair, axis=1).astype(BF16)
                )
        solved = jnp.dot(
            matrices.at[h].reshape(full, full)[...], right_side[h], preferred_element_type=F32
        ).astype(BF16)
        for o in range(n_rad):
            send_o[h, o] = solved[o * n_q:(o + 1) * n_q, :]

        def give(k, carry):
            peer = lax.rem(y + k, n_rad)
            pltpu.make_async_remote_copy(
                src_ref=send_o.at[h, peer], dst_ref=recv_o.at[h, y],
                send_sem=send4.at[h], recv_sem=recv4.at[h],
                device_id={"rad": peer}, device_id_type=MESH,
            ).start()
            return carry

        lax.fori_loop(1, n_rad, give, 0)
        recv_o[h, y] = send_o[h, y]

    flat_out = out_ref.reshape(n_t * n_q * 2, n_lat)
    for h in range(own):
        pltpu.make_async_copy(recv_o.at[h, others], recv_o.at[h, others], recv4.at[h]).wait()
        for o in range(n_rad):
            block_o = recv_o[h, o].astype(F32)
            for c in range(2):
                flat_out[pl.ds((o * own + h) * n_q * 2 + c, n_q, stride=2), :] = block_o[
                    :, c * n_lat:(c + 1) * n_lat
                ]

    left = inverse_hbm.at[pl.ds(0, (n_rad - 1) * own)]
    pltpu.make_async_copy(left, left, send0).wait()
    most = pl.ds(0, n_lat - 1)
    pltpu.make_async_copy(send_even.at[most], send_even.at[most], send1.at[0]).wait()
    pltpu.make_async_copy(send_odd.at[most], send_odd.at[most], send1.at[1]).wait()
    for h in range(own):
        pltpu.make_async_copy(send_c.at[h, most], send_c.at[h, most], send2.at[h]).wait()
        pltpu.make_async_copy(bring_c.at[h, others], bring_c.at[h, others], send3.at[h]).wait()
        pltpu.make_async_copy(send_o.at[h, others], send_o.at[h, others], send4.at[h]).wait()


def on_device(n_lat, n_rad, fourier, legendre, inverse, order_of_slot, degree_of_slot, degree_count):
    f, c, r, h, m, n_l = fourier.shape
    n_deg, n_h = legendre.shape[1:]
    n_t, n_q, full = inverse.shape
    own = n_t // n_rad
    rows = jnp.transpose(fourier, (0, 1, 2, 5, 3, 4)).reshape(f * c * r, n_l, h, m)
    block = min(LANES, n_deg)
    any_space = pl.BlockSpec(memory_space=pl.ANY)
    in_vmem = pl.BlockSpec(memory_space=pltpu.VMEM)
    dma = pltpu.SemaphoreType.DMA
    pairs = (n_lat, n_l // 2, 2, LANES)
    return pl.pallas_call(
        functools.partial(kernel, (n_lat, n_rad, n_l, n_deg, n_t)),
        out_shape=jax.ShapeDtypeStruct((n_t, n_q, c, n_lat), F32),
        in_specs=[in_vmem] * 3 + [any_space] * 3,
        out_specs=in_vmem,
        scratch_shapes=[
            pltpu.VMEM((n_l, f * c * r, h, m), BF16),
            pltpu.VMEM((n_deg, n_h), BF16),
            pltpu.VMEM((n_lat * n_l, LANES), F32),
            pltpu.VMEM((n_lat * n_l, LANES), F32),
            pltpu.VMEM(pairs, BF16),
            pltpu.VMEM(pairs, BF16),
            pltpu.VMEM(pairs, BF16),
            pltpu.VMEM(pairs, BF16),
            pltpu.VMEM((n_deg, LANES), F32),
            pltpu.VMEM((n_deg, n_deg), BF16),
            pltpu.VMEM((n_deg, LANES), F32),
            pltpu.VMEM((n_deg, n_h), BF16),
            pltpu.VMEM((own, n_lat, n_rad, LANES), BF16),
            pltpu.VMEM((own, n_lat, n_rad, LANES), BF16),
            pltpu.VMEM((own, n_lat * n_rad, LANES), F32),
            pltpu.VMEM((own, n_rad, n_lat, LANES), BF16),
            pltpu.VMEM((own, n_rad, n_lat, LANES), BF16),
            pltpu.VMEM((own, n_rad, n_q, full), BF16),
            pltpu.VMEM((own, full, c * n_lat), BF16),
            pltpu.VMEM((own, n_rad, n_q, c * n_lat), BF16),
            pltpu.VMEM((own, n_rad, n_q, c * n_lat), BF16),
            dma((n_l,)), dma, dma, dma,
            dma((2,)), dma((2,)), dma((own,)), dma((own,)),
            dma((own,)), dma((own,)), dma((own,)), dma((own,)),
        ],
        compiler_params=pltpu.CompilerParams(
            collective_id=0, has_side_effects=True, vmem_limit_bytes=56 << 20
        ),
    )(
        order_of_slot.reshape(1, n_lat),
        degree_of_slot.reshape(n_deg // block, block),
        degree_count.reshape(1, n_lat),
        rows,
        legendre.reshape(n_deg, n_h),
        inverse,
    )


def solution(mesh):
    in_specs = (
        P(None, None, "rad", None, None, "lat"),
        P("lat", None, None),
        P("lat", "rad", None),
        P(),
        P(),
        P(),
    )
    out_specs = P("lat", "rad", None, None)
    body = functools.partial(on_device, mesh.shape["lat"], mesh.shape["rad"])
    return jax.shard_map(
        body, mesh=mesh, in_specs=in_specs, out_specs=out_specs, check_vma=False
    )
```

time: 71.9 us -> 61.2 us (0.85); the launches traced: 71.7 us -> 60.2 us
  Pallas kernels: 69.4 us -> 57.9 us
    pallas_call x1, Pallas kernels: 69.4 us -> 57.9 us  [on_device(): pl.pallas_call(functools.partial(kernel, (n_lat, n_rad, n_l, n_deg, n_t))...]
where the time goes in v2:
time: 61.2 us; the launch traced here: 60.2 us
  Pallas kernels  57.9 us (95%)
  local copies, waits for them, and re-layouts  2.3 us (4%)
    pallas_call x1, Pallas kernels, on_device(): pl.pallas_call(functools.partial(kernel, (n_lat, n_rad, n_l, n_deg, n_t))...  57.9 us
    unnamed x1, local copies, waits for them, and re-layouts  2.3 us

profile of v2, /device:TPU:1, one launch (start us, length us, event | category | flops | bytes accessed | tf_op | source)
XLA Modules:
  0.0 60.2 jit_solution(94001241295714766)
XLA Ops:
  0.0 57.9 %shard_map.64 = f32[16,64,2,64]{3,2,1,0:T(2,128)} custom-call(s32[1,64]{1,0:T(1,128)} %bitcast.10, s32[8,128]{1,0:T(8,128)} %bitcast.9, s32[1,64]{1,0:T(1,128)} %bitcast.11, bf16[128,18,2,64]{3,2,1,0:T(2,128)(2,1)} %bitcast.8, bf16[1024,1152]{1,0:T(8,128)(2,1)} %bitcast.7, bf16[16,64,512]{2,1,0:T(8,128)(2,1)} %inverse_hbm.1), custom_call_target="tpu_custom_call" | custom-call | tf_op jit(solution)/shard_map/pallas_call | solution.py:301
  57.9 2.3 %copy.8 = f32[16,64,2,64]{3,2,1,0:T(2,128)} copy(f32[16,64,2,64]{3,2,1,0:T(2,128)} %shard_map.64) | data formatting | bytes 1048576

commit v3 on v2

v3 whole, which is shorter than its diff:
```python
import functools

import jax
import jax.numpy as jnp
from jax import lax
from jax.experimental import pallas as pl
from jax.experimental.pallas import tpu as pltpu
from jax.sharding import PartitionSpec as P

BF16 = jnp.bfloat16
F32 = jnp.float32
MESH = pl.DeviceIdType.MESH
LANES = 128


def iota(shape, dim):
    return lax.broadcasted_iota(jnp.int32, shape, dim)


def column(row):
    return jnp.transpose(jnp.broadcast_to(row, (LANES, row.shape[1])))


def dot_nt(a, b):
    return lax.dot_general(a, b, (((1,), (1,)), ((), ())), preferred_element_type=F32)


def farthest_first(k, n):
    return n // 2 + lax.select(lax.rem(k, 2) == 0, k // 2, -((k + 1) // 2))


def kernel(
    dims,
    order_hbm, degree_hbm, count_hbm, rows_hbm, table_hbm, inverse_hbm,
    recv_o,
    order_ref, degree_ref, count_ref, rows, table, north, south, send_folds, recv_folds,
    pick, column_degree, table_live, send_c, got_c, wide, matrices, right_side, send_o,
    small_sem, rows_sem, table_sem, send0, recv0, send1, recv1, send2, recv2, send4, recv4,
):
    n_lat, n_rad, n_l, n_deg, n_t = dims
    own = n_t // n_rad
    n_q, full = matrices.shape[2], matrices.shape[3]
    radii = full // 2 // n_rad
    me = lax.axis_index("lat")
    y = lax.axis_index("rad")
    group, planes = 8, n_lat // 8
    z, x, core = me // group, lax.rem(me, group) // 2, lax.rem(me, 2)
    places = [
        lax.rem(x + d, 4) * 2 + lax.rem(core + 1 + i, 2) for d in (2, 1, 3, 0) for i in range(2)
    ]

    def ring_of_planes(k):
        return lax.rem(z + farthest_first(k, planes), planes)

    def rad_peer(k):
        return lax.rem(y + farthest_first(k, n_rad), n_rad)

    smalls = [
        pltpu.make_async_copy(src, dst, small_sem.at[i])
        for i, (src, dst) in enumerate(
            ((order_hbm, order_ref), (degree_hbm, degree_ref), (count_hbm, count_ref))
        )
    ]

    def load_rows(l):
        return pltpu.make_async_copy(rows_hbm.at[:, l], rows.at[l], rows_sem.at[l])

    smalls[0].start()
    for l in range(n_l):
        load_rows(l).start()
    smalls[1].start()
    smalls[2].start()
    load_table = pltpu.make_async_copy(table_hbm, table, table_sem)
    load_table.start()

    barrier = pltpu.get_barrier_semaphore()

    def greet_lat(k, carry):
        plane = ring_of_planes(k)
        for place in places:
            pl.semaphore_signal(
                barrier, inc=1, device_id={"lat": plane * group + place}, device_id_type=MESH
            )
        return carry

    def greet_rad(k, carry):
        pl.semaphore_signal(
            barrier, inc=1, device_id={"rad": lax.rem(y + k, n_rad)}, device_id_type=MESH
        )
        return carry

    lax.fori_loop(0, planes - 1, greet_lat, 0)
    for place in places[:-1]:
        pl.semaphore_signal(
            barrier, inc=1, device_id={"lat": z * group + place}, device_id_type=MESH
        )
    lax.fori_loop(1, n_rad, greet_rad, 0)

    smalls[0].wait()
    order = order_ref[...].astype(F32)
    order_column = column(order)[:, :n_lat]
    order_pick = jnp.where(
        order_column == iota((n_lat, n_lat), 1).astype(F32), 1.0, 0.0
    ).astype(BF16)
    load_rows(0).wait()
    for l in range(1, n_l):
        load_rows(l).wait()
    for l in range(n_l):
        picked = dot_nt(order_pick, rows.at[l].reshape(2 * LANES, n_lat)[...])
        north[pl.ds(l, n_lat, stride=n_l), :] = picked[:, :LANES]
        south[pl.ds(l, n_lat, stride=n_l), :] = picked[:, LANES:]

    source, target = iota((2 * LANES, 2 * LANES), 0), iota((2 * LANES, 2 * LANES), 1)
    fold = jnp.where(
        source // 2 == target % LANES,
        jnp.where((source % 2 == 1) & (target >= LANES), -1.0, 1.0),
        0.0,
    ).astype(BF16)

    pl.semaphore_wait(barrier, n_lat + n_rad - 2)

    def send_matrices(k, carry):
        peer = rad_peer(k)
        pltpu.make_async_remote_copy(
            src_ref=inverse_hbm.at[pl.ds(peer * own, own)], dst_ref=matrices.at[:, y],
            send_sem=send0, recv_sem=recv0,
            device_id={"rad": peer}, device_id_type=MESH,
        ).start()
        return carry

    lax.fori_loop(0, n_rad - 1, send_matrices, 0)
    pltpu.make_async_copy(inverse_hbm.at[pl.ds(y * own, own)], matrices.at[:, y], recv0).start()

    def fold_and_send(plane, own_plane):
        at = pl.ds(pl.multiple_of(plane * (group * n_l), 16), group * n_l)
        both = jnp.concatenate([north[at, :], south[at, :]], axis=1).astype(BF16)
        folded = jnp.dot(both, fold, preferred_element_type=F32).astype(BF16)
        for p in range(2):
            send_folds.at[p].reshape(n_lat * n_l, LANES)[at, :] = folded[
                :, p * LANES:(p + 1) * LANES
            ]
        for place in places[:-1] if own_plane else places:
            peer = plane * group + place
            pltpu.make_async_remote_copy(
                src_ref=send_folds.at[:, peer], dst_ref=recv_folds.at[:, me],
                send_sem=send1, recv_sem=recv1,
                device_id={"lat": peer}, device_id_type=MESH,
            ).start()
        if own_plane:
            pltpu.make_async_copy(send_folds.at[:, me], recv_folds.at[:, me], recv1).start()

    def fold_other(k, carry):
        fold_and_send(ring_of_planes(k), False)
        return carry

    lax.fori_loop(0, planes - 1, fold_other, 0)
    fold_and_send(z, True)

    smalls[1].wait()
    smalls[2].wait()
    mine = jnp.sum(jnp.where(iota((1, n_lat), 1) == me, order, 0.0), axis=1, keepdims=True)
    count = jnp.sum(
        jnp.where(iota((1, n_lat), 1).astype(F32) == mine, count_ref[...].astype(F32), 0.0),
        axis=1, keepdims=True,
    )
    first = n_deg - count
    blocks, block = degree_ref.shape

    def pick_rows(b, carry):
        at = pl.ds(pl.multiple_of(b * block, block), block)
        held = column(degree_ref[pl.ds(b, 1), :].astype(F32))
        column_degree[at, :] = held
        cell = held[:, :block]
        for j in range(blocks):
            lane = (iota((block, block), 1) + j * block).astype(F32)
            pick[at, j * block:(j + 1) * block] = jnp.where(
                (cell == lane) & (cell >= first), 1.0, 0.0
            ).astype(BF16)
        return carry

    lax.fori_loop(0, blocks, pick_rows, 0)

    load_table.wait()
    rows_at_once = 2 * group * n_t

    def order_rows(b, carry):
        at = pl.ds(pl.multiple_of(b * rows_at_once, rows_at_once), rows_at_once)
        table_live[at, :] = jnp.dot(
            pick[at, :], table[...], preferred_element_type=F32
        ).astype(BF16)
        return carry

    lax.fori_loop(0, n_deg // rows_at_once, order_rows, 0)

    pltpu.make_async_copy(recv_folds, recv_folds, recv1).wait()

    def analyse(pair):
        at = pl.ds(pl.multiple_of(pair * rows_at_once, rows_at_once), rows_at_once)
        both = jnp.concatenate(
            [recv_folds.at[p].reshape(n_lat * n_l, LANES)[...] for p in range(2)], axis=1
        )
        product = jnp.dot(table_live[at, :], both, preferred_element_type=F32)
        parity = (column_degree[at, :] - first).astype(jnp.int32) & 1
        send_c.reshape(n_deg, LANES)[at, :] = jnp.where(
            parity == 0, product[:, :LANES], product[:, LANES:]
        ).astype(BF16)

    def send(peer, peer_y):
        pltpu.make_async_remote_copy(
            src_ref=send_c.at[peer, peer_y], dst_ref=got_c.at[y, me],
            send_sem=send2, recv_sem=recv2,
            device_id={"lat": peer, "rad": peer_y}, device_id_type=MESH,
        ).start()

    def send_pair(k, carry):
        pair = lax.rem(z // 2 + farthest_first(k, planes // 2), planes // 2)
        analyse(pair)

        def send_to(i, c):
            plane = pair * 2 + lax.rem(z + 1 + i // n_rad, 2)
            peer_y = rad_peer(lax.rem(i, n_rad))
            for place in places[:-1]:
                send(plane * group + place, peer_y)
            last = plane * group + places[-1]

            @pl.when((last != me) | (peer_y != y))
            def _():
                send(last, peer_y)

            return c

        lax.fori_loop(0, 2 * n_rad, send_to, 0)
        return carry

    lax.fori_loop(0, planes // 2, send_pair, 0)
    pltpu.make_async_copy(send_c.at[me, y], got_c.at[y, me], recv2).start()

    pltpu.make_async_copy(matrices, matrices, recv0).wait()
    pltpu.make_async_copy(got_c, got_c, recv2).wait()
    for o in range(n_rad):
        wide[o] = got_c.at[o].reshape(n_lat * own, LANES)[...].astype(F32)
    for h in range(own):
        for o in range(n_rad):
            turned = jnp.transpose(wide[o, pl.ds(h, n_lat, stride=own), :])
            for f in range(2):
                pair = [turned[(2 * f + c) * radii:(2 * f + c + 1) * radii, :] for c in range(2)]
                right_side[h, f * (full // 2) + o * radii:f * (full // 2) + (o + 1) * radii, :] = (
                    jnp.concatenate(pair, axis=1).astype(BF16)
                )
        solved = jnp.dot(
            matrices.at[h].reshape(full, full)[...], right_side[h], preferred_element_type=F32
        ).astype(BF16)
        for o in range(n_rad):
            send_o[h, o] = solved[o * n_q:(o + 1) * n_q, :]

        def give(k, carry):
            peer = rad_peer(k)
            pltpu.make_async_remote_copy(
                src_ref=send_o.at[h, peer], dst_ref=recv_o.at[h, y],
                send_sem=send4.at[h], recv_sem=recv4.at[h],
                device_id={"rad": peer}, device_id_type=MESH,
            ).start()
            return carry

        lax.fori_loop(0, n_rad - 1, give, 0)
        pltpu.make_async_copy(send_o.at[h, y], recv_o.at[h, y], recv4.at[h]).start()

    for h in range(own):
        pltpu.make_async_copy(recv_o.at[h], recv_o.at[h], recv4.at[h]).wait()

    left = inverse_hbm.at[pl.ds(0, (n_rad - 1) * own)]
    pltpu.make_async_copy(left, left, send0).wait()
    most = pl.ds(0, n_lat - 1)
    pltpu.make_async_copy(send_folds.at[:, most], send_folds.at[:, most], send1).wait()
    pltpu.make_async_copy(send_c.at[most], send_c.at[most], send2).wait()
    rest, others = send_c.at[0, pl.ds(0, n_rad - 1)], pl.ds(0, n_rad - 1)
    pltpu.make_async_copy(rest, rest, send2).wait()
    for h in range(own):
        pltpu.make_async_copy(send_o.at[h, others], send_o.at[h, others], send4.at[h]).wait()


def widen(solved_ref, out_ref):
    n_rad, n_q = solved_ref.shape[1:3]
    n_lat = out_ref.shape[4]
    for o in range(n_rad):
        flat = out_ref.at[o, 0].reshape(n_q * 2, n_lat)
        block = solved_ref[0, o].astype(F32)
        for c in range(2):
            flat[pl.ds(c, n_q, stride=2), :] = block[:, c * n_lat:(c + 1) * n_lat]


def on_device(n_lat, n_rad, fourier, legendre, inverse, order_of_slot, degree_of_slot, degree_count):
    f, c, r, h, m, n_l = fourier.shape
    n_deg, n_h = legendre.shape[1:]
    n_t, n_q, full = inverse.shape
    own = n_t // n_rad
    rows = jnp.transpose(fourier, (0, 1, 2, 5, 3, 4)).reshape(f * c * r, n_l, h, m)
    block = min(LANES, n_deg)
    any_space = pl.BlockSpec(memory_space=pl.ANY)
    dma = pltpu.SemaphoreType.DMA
    pairs = (2, n_lat, n_l // 2, 2, LANES)
    solved = pl.pallas_call(
        functools.partial(kernel, (n_lat, n_rad, n_l, n_deg, n_t)),
        out_shape=jax.ShapeDtypeStruct((own, n_rad, n_q, c * n_lat), BF16),
        in_specs=[any_space] * 6,
        out_specs=any_space,
        scratch_shapes=[
            pltpu.VMEM((1, n_lat), jnp.int32),
            pltpu.VMEM((n_deg // block, block), jnp.int32),
            pltpu.VMEM((1, n_lat), jnp.int32),
            pltpu.VMEM((n_l, f * c * r, h, m), BF16),
            pltpu.VMEM((n_deg, n_h), BF16),
            pltpu.VMEM((n_lat * n_l, LANES), F32),
            pltpu.VMEM((n_lat * n_l, LANES), F32),
            pltpu.VMEM(pairs, BF16),
            pltpu.VMEM(pairs, BF16),
            pltpu.VMEM((n_deg, n_deg), BF16),
            pltpu.VMEM((n_deg, LANES), F32),
            pltpu.VMEM((n_deg, n_h), BF16),
            pltpu.VMEM((n_lat, n_rad, own, LANES), BF16),
            pltpu.VMEM((n_rad, n_lat, own, LANES), BF16),
            pltpu.VMEM((n_rad, n_lat * own, LANES), F32),
            pltpu.VMEM((own, n_rad, n_q, full), BF16),
            pltpu.VMEM((own, full, c * n_lat), BF16),
            pltpu.VMEM((own, n_rad, n_q, c * n_lat), BF16),
            dma((3,)), dma((n_l,)), dma, dma, dma,
            dma, dma, dma, dma, dma((own,)), dma((own,)),
        ],
        compiler_params=pltpu.CompilerParams(
            collective_id=0, has_side_effects=True, vmem_limit_bytes=56 << 20
        ),
    )(
        order_of_slot.reshape(1, n_lat),
        degree_of_slot.reshape(n_deg // block, block),
        degree_count.reshape(1, n_lat),
        rows,
        legendre.reshape(n_deg, n_h),
        inverse,
    )
    return pl.pallas_call(
        widen,
        grid=(own,),
        out_shape=jax.ShapeDtypeStruct((n_rad, own, n_q, c, n_lat), F32),
        in_specs=[pl.BlockSpec((1, n_rad, n_q, c * n_lat), lambda i: (i, 0, 0, 0))],
        out_specs=pl.BlockSpec((n_rad, 1, n_q, c, n_lat), lambda i: (0, i, 0, 0, 0)),
    )(solved).reshape(n_t, n_q, c, n_lat)


def solution(mesh):
    in_specs = (
        P(None, None, "rad", None, None, "lat"),
        P("lat", None, None),
        P("lat", "rad", None),
        P(),
        P(),
        P(),
    )
    out_specs = P("lat", "rad", None, None)
    body = functools.partial(on_device, mesh.shape["lat"], mesh.shape["rad"])
    return jax.shard_map(
        body, mesh=mesh, in_specs=in_specs, out_specs=out_specs, check_vma=False
    )
```

time: 61.2 us -> 60.5 us (0.989); the launches traced: 60.2 us -> 60.4 us
  Pallas kernels: 57.9 us -> 60.4 us
  local copies, waits for them, and re-layouts: 2.3 us -> 0 us
    unnamed x1 -> x0, local copies, waits for them, and re-layouts: 2.3 us -> none
    pallas_call x0 -> x1, Pallas kernels: none -> 1.98 us  [on_device(): pl.pallas_call(widen, grid=(own,), out_shape=jax.ShapeDtypeStruct((n_rad,...]
where the time goes in v3:
time: 60.5 us; the launch traced here: 60.4 us
  Pallas kernels  60.4 us (100%)
    pallas_call x1, Pallas kernels, on_device(): pl.pallas_call(functools.partial(kernel, (n_lat, n_rad, n_l, n_deg, n_t))...  58.4 us
    pallas_call x1, Pallas kernels, on_device(): pl.pallas_call(widen, grid=(own,), out_shape=jax.ShapeDtypeStruct((n_rad,...  1.98 us

profile of v3, /device:TPU:1, one launch (start us, length us, event | category | flops | bytes accessed | tf_op | source)
XLA Modules:
  0.0 60.4 jit_solution(10138731477741461678)
XLA Ops:
  0.0 58.4 %shard_map.64.solved_ref = bf16[2,8,64,128]{3,2,1,0:T(8,128)(2,1)} custom-call(s32[1,64]{1,0:T(1,128)} %bitcast.11, s32[8,128]{1,0:T(8,128)} %bitcast.10, s32[1,64]{1,0:T(1,128)} %bitcast.12, bf16[128,18,2,64]{3,2,1,0:T(2,128)(2,1)} %bitcast.9, bf16[1024,1152]{1,0:T(8,128)(2,1)} %bitcast.8, bf16[16,64,512]{2,1,0:T(8,128)(2,1)} %inverse_hbm.1), custom_call_target="tpu_custom_call" | custom-call | tf_op jit(solution)/shard_map/pallas_call | solution.py:302
  58.4 2.0 %shard_map.65 = f32[8,2,64,2,64]{4,3,2,1,0:T(2,128)} custom-call(bf16[2,8,64,128]{3,2,1,0:T(8,128)(2,1)} %shard_map.64.solved_ref), custom_call_target="tpu_custom_call" | custom-call | tf_op jit(solution)/shard_map/pallas_call | solution.py:340

commit v4 on v3

--- a/solution.py
+++ b/solution.py
@@ -11,6 +11,7 @@
 F32 = jnp.float32
 MESH = pl.DeviceIdType.MESH
 LANES = 128
+PIECES = 2
 
 
 def iota(shape, dim):
@@ -34,8 +35,9 @@
     order_hbm, degree_hbm, count_hbm, rows_hbm, table_hbm, inverse_hbm,
     recv_o,
     order_ref, degree_ref, count_ref, rows, table, north, south, send_folds, recv_folds,
-    pick, column_degree, table_live, send_c, got_c, wide, matrices, right_side, send_o,
-    small_sem, rows_sem, table_sem, send0, recv0, send1, recv1, send2, recv2, send4, recv4,
+    natural_degree, pick, column_degree, table_live, send_c, recv_c, wide,
+    bring_c, got_c, matrices, right_side, send_o,
+    small_sem, rows_sem, table_sem, send0, recv0, send1, recv1, send2, recv2, send3, recv3, send4, recv4,
 ):
     n_lat, n_rad, n_l, n_deg, n_t = dims
     own = n_t // n_rad
@@ -166,22 +168,31 @@
     first = n_deg - count
     blocks, block = degree_ref.shape
 
-    def pick_rows(b, carry):
+    def to_column(b, carry):
         at = pl.ds(pl.multiple_of(b * block, block), block)
-        held = column(degree_ref[pl.ds(b, 1), :].astype(F32))
-        column_degree[at, :] = held
-        cell = held[:, :block]
-        for j in range(blocks):
-            lane = (iota((block, block), 1) + j * block).astype(F32)
-            pick[at, j * block:(j + 1) * block] = jnp.where(
-                (cell == lane) & (cell >= first), 1.0, 0.0
-            ).astype(BF16)
-        return carry
-
-    lax.fori_loop(0, blocks, pick_rows, 0)
+        natural_degree[at, :] = column(degree_ref[pl.ds(b, 1), :].astype(F32))
+        return carry
+
+    lax.fori_loop(0, blocks, to_column, 0)
+    step = n_deg // own // blocks
+
+    for h in range(own):
+        def pick_rows(b, carry):
+            held = natural_degree[pl.ds(b * (step * own) + h, step, stride=own), :]
+            at = pl.ds(pl.multiple_of(b * step + h * (n_deg // own), step), step)
+            column_degree[at, :] = held
+            for j in range(blocks):
+                lane = (iota((step, block), 1) + j * block).astype(F32)
+                cell = held[:, :block]
+                pick[at, j * block:(j + 1) * block] = jnp.where(
+                    (cell == lane) & (cell >= first), 1.0, 0.0
+                ).astype(BF16)
+            return carry
+
+        lax.fori_loop(0, blocks, pick_rows, 0)
 
     load_table.wait()
-    rows_at_once = 2 * group * n_t
+    rows_at_once = min(256, n_deg // own)
 
     def order_rows(b, carry):
         at = pl.ds(pl.multiple_of(b * rows_at_once, rows_at_once), rows_at_once)
@@ -194,99 +205,145 @@
 
     pltpu.make_async_copy(recv_folds, recv_folds, recv1).wait()
 
-    def analyse(pair):
-        at = pl.ds(pl.multiple_of(pair * rows_at_once, rows_at_once), rows_at_once)
-        both = jnp.concatenate(
-            [recv_folds.at[p].reshape(n_lat * n_l, LANES)[...] for p in range(2)], axis=1
-        )
-        product = jnp.dot(table_live[at, :], both, preferred_element_type=F32)
-        parity = (column_degree[at, :] - first).astype(jnp.int32) & 1
-        send_c.reshape(n_deg, LANES)[at, :] = jnp.where(
-            parity == 0, product[:, :LANES], product[:, LANES:]
-        ).astype(BF16)
-
-    def send(peer, peer_y):
-        pltpu.make_async_remote_copy(
-            src_ref=send_c.at[peer, peer_y], dst_ref=got_c.at[y, me],
-            send_sem=send2, recv_sem=recv2,
-            device_id={"lat": peer, "rad": peer_y}, device_id_type=MESH,
-        ).start()
-
-    def send_pair(k, carry):
-        pair = lax.rem(z // 2 + farthest_first(k, planes // 2), planes // 2)
-        analyse(pair)
-
-        def send_to(i, c):
-            plane = pair * 2 + lax.rem(z + 1 + i // n_rad, 2)
-            peer_y = rad_peer(lax.rem(i, n_rad))
-            for place in places[:-1]:
-                send(plane * group + place, peer_y)
-            last = plane * group + places[-1]
-
-            @pl.when((last != me) | (peer_y != y))
-            def _():
-                send(last, peer_y)
-
-            return c
-
-        lax.fori_loop(0, 2 * n_rad, send_to, 0)
-        return carry
-
-    lax.fori_loop(0, planes // 2, send_pair, 0)
-    pltpu.make_async_copy(send_c.at[me, y], got_c.at[y, me], recv2).start()
+    parts = n_deg // own // rows_at_once
+
+    reach = planes // parts
+
+    for h in range(own):
+        def send(peer):
+            pltpu.make_async_remote_copy(
+                src_ref=send_c.at[h, peer], dst_ref=recv_c.at[h, me],
+                send_sem=send2.at[h], recv_sem=recv2.at[h],
+                device_id={"lat": peer}, device_id_type=MESH,
+            ).start()
+
+        def analyse_and_send(k, carry):
+            part = lax.rem(z // reach + 1 + k, parts)
+            begin = pl.multiple_of(part * rows_at_once, rows_at_once)
+            at = pl.ds(begin + h * (n_deg // own), rows_at_once)
+            both = jnp.concatenate(
+                [recv_folds.at[p].reshape(n_lat * n_l, LANES)[...] for p in range(2)], axis=1
+            )
+            product = jnp.dot(table_live[at, :], both, preferred_element_type=F32)
+            parity = (column_degree[at, :] - first).astype(jnp.int32) & 1
+            send_c.at[h].reshape(n_lat * n_rad, LANES)[pl.ds(begin, rows_at_once), :] = jnp.where(
+                parity == 0, product[:, :LANES], product[:, LANES:]
+            ).astype(BF16)
+
+            def send_plane(j, c):
+                plane = part * reach + lax.rem(z + 1 + j, reach)
+                for place in places[:-1]:
+                    send(plane * group + place)
+                last = plane * group + places[-1]
+
+                @pl.when(last != me)
+                def _():
+                    send(last)
+
+                return c
+
+            return lax.fori_loop(0, reach, send_plane, carry)
+
+        lax.fori_loop(0, parts, analyse_and_send, 0)
+        pltpu.make_async_copy(send_c.at[h, me], recv_c.at[h, me], recv2.at[h]).start()
+
+    some = n_lat // PIECES
+    for h in range(own):
+        pltpu.make_async_copy(recv_c.at[h], recv_c.at[h], recv2.at[h]).wait()
+        wide[h] = recv_c.at[h].reshape(n_lat * n_rad, LANES)[...].astype(F32)
+        for p in range(PIECES):
+            def bring(k, carry):
+                peer = rad_peer(k)
+                bring_c[h, p, peer] = wide[
+                    h, pl.ds(p * some * n_rad + peer, some, stride=n_rad), :
+                ].astype(BF16)
+                pltpu.make_async_remote_copy(
+                    src_ref=bring_c.at[h, p, peer], dst_ref=got_c.at[h, p, y],
+                    send_sem=send3.at[h, p], recv_sem=recv3.at[h, p],
+                    device_id={"rad": peer}, device_id_type=MESH,
+                ).start()
+                return carry
+
+            lax.fori_loop(0, n_rad - 1, bring, 0)
+            got_c[h, p, y] = wide[
+                h, pl.ds(p * some * n_rad + y, some, stride=n_rad), :
+            ].astype(BF16)
 
     pltpu.make_async_copy(matrices, matrices, recv0).wait()
-    pltpu.make_async_copy(got_c, got_c, recv2).wait()
-    for o in range(n_rad):
-        wide[o] = got_c.at[o].reshape(n_lat * own, LANES)[...].astype(F32)
-    for h in range(own):
-        for o in range(n_rad):
-            turned = jnp.transpose(wide[o, pl.ds(h, n_lat, stride=own), :])
-            for f in range(2):
-                pair = [turned[(2 * f + c) * radii:(2 * f + c + 1) * radii, :] for c in range(2)]
-                right_side[h, f * (full // 2) + o * radii:f * (full // 2) + (o + 1) * radii, :] = (
-                    jnp.concatenate(pair, axis=1).astype(BF16)
-                )
-        solved = jnp.dot(
-            matrices.at[h].reshape(full, full)[...], right_side[h], preferred_element_type=F32
-        ).astype(BF16)
-        for o in range(n_rad):
-            send_o[h, o] = solved[o * n_q:(o + 1) * n_q, :]
-
-        def give(k, carry):
-            peer = rad_peer(k)
-            pltpu.make_async_remote_copy(
-                src_ref=send_o.at[h, peer], dst_ref=recv_o.at[h, y],
-                send_sem=send4.at[h], recv_sem=recv4.at[h],
-                device_id={"rad": peer}, device_id_type=MESH,
+    others = pl.ds(0, n_rad - 1)
+    slab = n_q // PIECES
+    for h in range(own):
+        for p in range(PIECES):
+            pltpu.make_async_copy(
+                got_c.at[h, p, others], got_c.at[h, p, others], recv3.at[h, p]
+            ).wait()
+            for o in range(n_rad):
+                turned = jnp.transpose(got_c[h, p, o].astype(F32))
+                for f in range(2):
+                    pair = [
+                        turned[(2 * f + c) * radii:(2 * f + c + 1) * radii, :] for c in range(2)
+                    ]
+                    begin = f * (full // 2) + o * radii
+                    right_side[h, p, begin:begin + radii, :] = jnp.concatenate(
+                        pair, axis=1
+                    ).astype(BF16)
+            solved = jnp.dot(
+                matrices.at[h].reshape(full, full)[...], right_side[h, p],
+                preferred_element_type=F32,
+            )
+            for o in range(n_rad):
+                send_o[h, p, o] = jnp.concatenate(
+                    [
+                        solved[o * n_q + i * slab:o * n_q + (i + 1) * slab, :]
+                        for i in range(PIECES)
+                    ],
+                    axis=1,
+                ).astype(BF16)
+
+            def give(k, carry):
+                peer = rad_peer(k)
+                pltpu.make_async_remote_copy(
+                    src_ref=send_o.at[h, p, peer], dst_ref=recv_o.at[h, p, y],
+                    send_sem=send4.at[h, p], recv_sem=recv4.at[h, p],
+                    device_id={"rad": peer}, device_id_type=MESH,
+                ).start()
+                return carry
+
+            lax.fori_loop(0, n_rad - 1, give, 0)
+            pltpu.make_async_copy(
+                send_o.at[h, p, y], recv_o.at[h, p, y], recv4.at[h, p]
             ).start()
-            return carry
-
-        lax.fori_loop(0, n_rad - 1, give, 0)
-        pltpu.make_async_copy(send_o.at[h, y], recv_o.at[h, y], recv4.at[h]).start()
-
-    for h in range(own):
-        pltpu.make_async_copy(recv_o.at[h], recv_o.at[h], recv4.at[h]).wait()
+
+    for h in range(own):
+        for p in range(PIECES):
+            pltpu.make_async_copy(recv_o.at[h, p], recv_o.at[h, p], recv4.at[h, p]).wait()
 
     left = inverse_hbm.at[pl.ds(0, (n_rad - 1) * own)]
     pltpu.make_async_copy(left, left, send0).wait()
     most = pl.ds(0, n_lat - 1)
     pltpu.make_async_copy(send_folds.at[:, most], send_folds.at[:, most], send1).wait()
-    pltpu.make_async_copy(send_c.at[most], send_c.at[most], send2).wait()
-    rest, others = send_c.at[0, pl.ds(0, n_rad - 1)], pl.ds(0, n_rad - 1)
-    pltpu.make_async_copy(rest, rest, send2).wait()
-    for h in range(own):
-        pltpu.make_async_copy(send_o.at[h, others], send_o.at[h, others], send4.at[h]).wait()
+    for h in range(own):
+        pltpu.make_async_copy(send_c.at[h, most], send_c.at[h, most], send2.at[h]).wait()
+        for p in range(PIECES):
+            sent = bring_c.at[h, p, others]
+            pltpu.make_async_copy(sent, sent, send3.at[h, p]).wait()
+            sent = send_o.at[h, p, others]
+            pltpu.make_async_copy(sent, sent, send4.at[h, p]).wait()
 
 
 def widen(solved_ref, out_ref):
-    n_rad, n_q = solved_ref.shape[1:3]
-    n_lat = out_ref.shape[4]
+    n_rad, slab = solved_ref.shape[2:4]
+    n_q, n_c, n_lat = out_ref.shape[2:]
+    some = n_lat // PIECES
     for o in range(n_rad):
-        flat = out_ref.at[o, 0].reshape(n_q * 2, n_lat)
-        block = solved_ref[0, o].astype(F32)
-        for c in range(2):
-            flat[pl.ds(c, n_q, stride=2), :] = block[:, c * n_lat:(c + 1) * n_lat]
+        flat = out_ref.at[o, 0].reshape(n_q * n_c, n_lat)
+        block = [solved_ref[0, p, o].astype(F32) for p in range(PIECES)]
+        for i in range(PIECES):
+            for c in range(n_c):
+                begin = (i * n_c + c) * some
+                flat[pl.ds(i * slab * n_c + c, slab, stride=n_c), :] = jnp.concatenate(
+                    [b[:, begin:begin + some] for b in block], axis=1
+                )
 
 
 def on_device(n_lat, n_rad, fourier, legendre, inverse, order_of_slot, degree_of_slot, degree_count):
@@ -301,7 +358,7 @@
     pairs = (2, n_lat, n_l // 2, 2, LANES)
     solved = pl.pallas_call(
         functools.partial(kernel, (n_lat, n_rad, n_l, n_deg, n_t)),
-        out_shape=jax.ShapeDtypeStruct((own, n_rad, n_q, c * n_lat), BF16),
+        out_shape=jax.ShapeDtypeStruct((own, PIECES, n_rad, n_q // PIECES, c * n_lat), BF16),
         in_specs=[any_space] * 6,
         out_specs=any_space,
         scratch_shapes=[
@@ -314,17 +371,21 @@
             pltpu.VMEM((n_lat * n_l, LANES), F32),
             pltpu.VMEM(pairs, BF16),
             pltpu.VMEM(pairs, BF16),
+            pltpu.VMEM((n_deg, LANES), F32),
             pltpu.VMEM((n_deg, n_deg), BF16),
             pltpu.VMEM((n_deg, LANES), F32),
             pltpu.VMEM((n_deg, n_h), BF16),
-            pltpu.VMEM((n_lat, n_rad, own, LANES), BF16),
-            pltpu.VMEM((n_rad, n_lat, own, LANES), BF16),
-            pltpu.VMEM((n_rad, n_lat * own, LANES), F32),
+            pltpu.VMEM((own, n_lat, n_rad, LANES), BF16),
+            pltpu.VMEM((own, n_lat, n_rad, LANES), BF16),
+            pltpu.VMEM((own, n_lat * n_rad, LANES), F32),
+            pltpu.VMEM((own, PIECES, n_rad, n_lat // PIECES, LANES), BF16),
+            pltpu.VMEM((own, PIECES, n_rad, n_lat // PIECES, LANES), BF16),
             pltpu.VMEM((own, n_rad, n_q, full), BF16),
-            pltpu.VMEM((own, full, c * n_lat), BF16),
-            pltpu.VMEM((own, n_rad, n_q, c * n_lat), BF16),
+            pltpu.VMEM((own, PIECES, full, c * n_lat // PIECES), BF16),
+            pltpu.VMEM((own, PIECES, n_rad, n_q // PIECES, c * n_lat), BF16),
             dma((3,)), dma((n_l,)), dma, dma, dma,
-            dma, dma, dma, dma, dma((own,)), dma((own,)),
+            dma, dma, dma((own,)), dma((own,)),
+            dma((own, PIECES)), dma((own, PIECES)), dma((own, PIECES)), dma((own, PIECES)),
         ],
         compiler_params=pltpu.CompilerParams(
             collective_id=0, has_side_effects=True, vmem_limit_bytes=56 << 20
@@ -341,7 +402,11 @@
         widen,
         grid=(own,),
         out_shape=jax.ShapeDtypeStruct((n_rad, own, n_q, c, n_lat), F32),
-        in_specs=[pl.BlockSpec((1, n_rad, n_q, c * n_lat), lambda i: (i, 0, 0, 0))],
+        in_specs=[
+            pl.BlockSpec(
+                (1, PIECES, n_rad, n_q // PIECES, c * n_lat), lambda i: (i, 0, 0, 0, 0)
+            )
+        ],
         out_specs=pl.BlockSpec((n_rad, 1, n_q, c, n_lat), lambda i: (0, i, 0, 0, 0)),
     )(solved).reshape(n_t, n_q, c, n_lat)
 

time: 60.5 us -> 55.6 us (0.919)
  Pallas kernels: 60.4 us -> 55.2 us
    pallas_call x1, Pallas kernels: 58.4 us -> 53.1 us  [on_device(): pl.pallas_call(functools.partial(kernel, (n_lat, n_rad, n_l, n_deg, n_t))...]
where the time goes in v4:
time: 55.6 us; the launch traced here: 55.2 us
  Pallas kernels  55.2 us (99%)
    pallas_call x1, Pallas kernels, on_device(): pl.pallas_call(functools.partial(kernel, (n_lat, n_rad, n_l, n_deg, n_t))...  53.1 us
    pallas_call x1, Pallas kernels, on_device(): pl.pallas_call(widen, grid=(own,), out_shape=jax.ShapeDtypeStruct((n_rad,...  2.07 us

profile of v4, /device:TPU:1, one launch (start us, length us, event | category | flops | bytes accessed | tf_op | source)
XLA Modules:
  0.0 55.2 jit_solution(1190660821017579973)
XLA Ops:
  0.0 53.1 %shard_map.64.solved_ref = bf16[2,2,8,32,128]{4,3,2,1,0:T(8,128)(2,1)} custom-call(s32[1,64]{1,0:T(1,128)} %bitcast.11, s32[8,128]{1,0:T(8,128)} %bitcast.10, s32[1,64]{1,0:T(1,128)} %bitcast.12, bf16[128,18,2,64]{3,2,1,0:T(2,128)(2,1)} %bitcast.9, bf16[1024,1152]{1,0:T(8,128)(2,1)} %bitcast.8, bf16[16,64,512]{2,1,0:T(8,128)(2,1)} %inverse_hbm.1), custom_call_target="tpu_custom_call" | custom-call | tf_op jit(solution)/shard_map/pallas_call | solution.py:359
  53.1 2.1 %shard_map.65 = f32[8,2,64,2,64]{4,3,2,1,0:T(2,128)} custom-call(bf16[2,2,8,32,128]{4,3,2,1,0:T(8,128)(2,1)} %shard_map.64.solved_ref), custom_call_target="tpu_custom_call" | custom-call | tf_op jit(solution)/shard_map/pallas_call | solution.py:401

commit v5 on v4

--- a/solution.py
+++ b/solution.py
@@ -27,6 +27,8 @@
 
 
 def farthest_first(k, n):
+    if isinstance(k, int):
+        return n // 2 + (-((k + 1) // 2) if k % 2 else k // 2)
     return n // 2 + lax.select(lax.rem(k, 2) == 0, k // 2, -((k + 1) // 2))
 
 
@@ -119,7 +121,34 @@
         0.0,
     ).astype(BF16)
 
+    def fold_plane(k, carry):
+        at = pl.ds(pl.multiple_of(k * (2 * group * n_l), 16), 2 * group * n_l)
+        both = jnp.concatenate([north[at, :], south[at, :]], axis=1).astype(BF16)
+        folded = jnp.dot(both, fold, preferred_element_type=F32).astype(BF16)
+        for p in range(2):
+            send_folds.at[p].reshape(n_lat * n_l, LANES)[at, :] = folded[
+                :, p * LANES:(p + 1) * LANES
+            ]
+        return carry
+
+    lax.fori_loop(0, planes // 2, fold_plane, 0)
+
     pl.semaphore_wait(barrier, n_lat + n_rad - 2)
+
+    def send_folded(peer):
+        pltpu.make_async_remote_copy(
+            src_ref=send_folds.at[:, peer], dst_ref=recv_folds.at[:, me],
+            send_sem=send1, recv_sem=recv1,
+            device_id={"lat": peer}, device_id_type=MESH,
+        ).start()
+
+    for k in range(planes - 1):
+        plane = ring_of_planes(k)
+        for place in places:
+            send_folded(plane * group + place)
+    for place in places[:-1]:
+        send_folded(z * group + place)
+    pltpu.make_async_copy(send_folds.at[:, me], recv_folds.at[:, me], recv1).start()
 
     def send_matrices(k, carry):
         peer = rad_peer(k)
@@ -132,31 +161,6 @@
 
     lax.fori_loop(0, n_rad - 1, send_matrices, 0)
     pltpu.make_async_copy(inverse_hbm.at[pl.ds(y * own, own)], matrices.at[:, y], recv0).start()
-
-    def fold_and_send(plane, own_plane):
-        at = pl.ds(pl.multiple_of(plane * (group * n_l), 16), group * n_l)
-        both = jnp.concatenate([north[at, :], south[at, :]], axis=1).astype(BF16)
-        folded = jnp.dot(both, fold, preferred_element_type=F32).astype(BF16)
-        for p in range(2):
-            send_folds.at[p].reshape(n_lat * n_l, LANES)[at, :] = folded[
-                :, p * LANES:(p + 1) * LANES
-            ]
-        for place in places[:-1] if own_plane else places:
-            peer = plane * group + place
-            pltpu.make_async_remote_copy(
-                src_ref=send_folds.at[:, peer], dst_ref=recv_folds.at[:, me],
-                send_sem=send1, recv_sem=recv1,
-                device_id={"lat": peer}, device_id_type=MESH,
-            ).start()
-        if own_plane:
-            pltpu.make_async_copy(send_folds.at[:, me], recv_folds.at[:, me], recv1).start()
-
-    def fold_other(k, carry):
-        fold_and_send(ring_of_planes(k), False)
-        return carry
-
-    lax.fori_loop(0, planes - 1, fold_other, 0)
-    fold_and_send(z, True)
 
     smalls[1].wait()
     smalls[2].wait()
@@ -230,19 +234,16 @@
                 parity == 0, product[:, :LANES], product[:, LANES:]
             ).astype(BF16)
 
-            def send_plane(j, c):
+            for j in range(reach):
                 plane = part * reach + lax.rem(z + 1 + j, reach)
                 for place in places[:-1]:
                     send(plane * group + place)
                 last = plane * group + places[-1]
-
-                @pl.when(last != me)
-                def _():
+                if j < reach - 1:
                     send(last)
-
-                return c
-
-            return lax.fori_loop(0, reach, send_plane, carry)
+                else:
+                    pl.when(last != me)(functools.partial(send, last))
+            return carry
 
         lax.fori_loop(0, parts, analyse_and_send, 0)
         pltpu.make_async_copy(send_c.at[h, me], recv_c.at[h, me], recv2.at[h]).start()
@@ -272,32 +273,34 @@
     pltpu.make_async_copy(matrices, matrices, recv0).wait()
     others = pl.ds(0, n_rad - 1)
     slab = n_q // PIECES
+    lanes_of = iota((radii, LANES), 1)
+    second_part = lax.rem(lanes_of // some, 2) == 1
+    second_half = iota((slab, LANES), 1) >= LANES // PIECES
     for h in range(own):
         for p in range(PIECES):
             pltpu.make_async_copy(
                 got_c.at[h, p, others], got_c.at[h, p, others], recv3.at[h, p]
             ).wait()
             for o in range(n_rad):
-                turned = jnp.transpose(got_c[h, p, o].astype(F32))
+                block = got_c[h, p, o].astype(F32)
+                turned = jnp.transpose(jnp.concatenate([block] * (2 * PIECES), axis=0))
                 for f in range(2):
-                    pair = [
-                        turned[(2 * f + c) * radii:(2 * f + c + 1) * radii, :] for c in range(2)
-                    ]
+                    at = 2 * f * radii
                     begin = f * (full // 2) + o * radii
-                    right_side[h, p, begin:begin + radii, :] = jnp.concatenate(
-                        pair, axis=1
+                    right_side[h, p, begin:begin + radii, :] = jnp.where(
+                        second_part,
+                        turned[at + radii:at + 2 * radii, :],
+                        turned[at:at + radii, :],
                     ).astype(BF16)
             solved = jnp.dot(
                 matrices.at[h].reshape(full, full)[...], right_side[h, p],
                 preferred_element_type=F32,
             )
             for o in range(n_rad):
-                send_o[h, p, o] = jnp.concatenate(
-                    [
-                        solved[o * n_q + i * slab:o * n_q + (i + 1) * slab, :]
-                        for i in range(PIECES)
-                    ],
-                    axis=1,
+                send_o[h, p, o] = jnp.where(
+                    second_half,
+                    solved[o * n_q + slab:o * n_q + 2 * slab, :],
+                    solved[o * n_q:o * n_q + slab, :],
                 ).astype(BF16)
 
             def give(k, carry):
@@ -381,7 +384,7 @@
             pltpu.VMEM((own, PIECES, n_rad, n_lat // PIECES, LANES), BF16),
             pltpu.VMEM((own, PIECES, n_rad, n_lat // PIECES, LANES), BF16),
             pltpu.VMEM((own, n_rad, n_q, full), BF16),
-            pltpu.VMEM((own, PIECES, full, c * n_lat // PIECES), BF16),
+            pltpu.VMEM((own, PIECES, full, c * n_lat), BF16),
             pltpu.VMEM((own, PIECES, n_rad, n_q // PIECES, c * n_lat), BF16),
             dma((3,)), dma((n_l,)), dma, dma, dma,
             dma, dma, dma((own,)), dma((own,)),

time: 55.6 us -> 55.7 us (level)
  no operation moved by 1% of the time
where the time goes in v5:
time: 55.7 us; the launch traced here: 55.3 us
  Pallas kernels  55.3 us (99%)
    pallas_call x1, Pallas kernels, on_device(): pl.pallas_call(functools.partial(kernel, (n_lat, n_rad, n_l, n_deg, n_t))...  53.2 us
    pallas_call x1, Pallas kernels, on_device(): pl.pallas_call(widen, grid=(own,), out_shape=jax.ShapeDtypeStruct((n_rad,...  2.07 us

profile of v5, /device:TPU:1, one launch (start us, length us, event | category | flops | bytes accessed | tf_op | source)
XLA Modules:
  0.0 55.3 jit_solution(5330611712854335021)
XLA Ops:
  0.0 53.2 %shard_map.64.solved_ref = bf16[2,2,8,32,128]{4,3,2,1,0:T(8,128)(2,1)} custom-call(s32[1,64]{1,0:T(1,128)} %bitcast.11, s32[8,128]{1,0:T(8,128)} %bitcast.10, s32[1,64]{1,0:T(1,128)} %bitcast.12, bf16[128,18,2,64]{3,2,1,0:T(2,128)(2,1)} %bitcast.9, bf16[1024,1152]{1,0:T(8,128)(2,1)} %bitcast.8, bf16[16,64,512]{2,1,0:T(8,128)(2,1)} %inverse_hbm.1), custom_call_target="tpu_custom_call" | custom-call | tf_op jit(solution)/shard_map/pallas_call | solution.py:362
  53.2 2.1 %shard_map.65 = f32[8,2,64,2,64]{4,3,2,1,0:T(2,128)} custom-call(bf16[2,2,8,32,128]{4,3,2,1,0:T(8,128)(2,1)} %shard_map.64.solved_ref), custom_call_target="tpu_custom_call" | custom-call | tf_op jit(solution)/shard_map/pallas_call | solution.py:404

commit v6 on v5

--- a/solution.py
+++ b/solution.py
@@ -34,9 +34,9 @@
 
 def kernel(
     dims,
-    order_hbm, degree_hbm, count_hbm, rows_hbm, table_hbm, inverse_hbm,
+    small_hbm, rows_hbm, table_hbm, inverse_hbm,
     recv_o,
-    order_ref, degree_ref, count_ref, rows, table, north, south, send_folds, recv_folds,
+    small, rows, table, north, south, send_folds, recv_folds,
     natural_degree, pick, column_degree, table_live, send_c, recv_c, wide,
     bring_c, got_c, matrices, right_side, send_o,
     small_sem, rows_sem, table_sem, send0, recv0, send1, recv1, send2, recv2, send3, recv3, send4, recv4,
@@ -59,21 +59,14 @@
     def rad_peer(k):
         return lax.rem(y + farthest_first(k, n_rad), n_rad)
 
-    smalls = [
-        pltpu.make_async_copy(src, dst, small_sem.at[i])
-        for i, (src, dst) in enumerate(
-            ((order_hbm, order_ref), (degree_hbm, degree_ref), (count_hbm, count_ref))
-        )
-    ]
+    load_small = pltpu.make_async_copy(small_hbm, small, small_sem)
 
     def load_rows(l):
         return pltpu.make_async_copy(rows_hbm.at[:, l], rows.at[l], rows_sem.at[l])
 
-    smalls[0].start()
+    load_small.start()
     for l in range(n_l):
         load_rows(l).start()
-    smalls[1].start()
-    smalls[2].start()
     load_table = pltpu.make_async_copy(table_hbm, table, table_sem)
     load_table.start()
 
@@ -100,8 +93,8 @@
         )
     lax.fori_loop(1, n_rad, greet_rad, 0)
 
-    smalls[0].wait()
-    order = order_ref[...].astype(F32)
+    load_small.wait()
+    order = small[0:1, :n_lat].astype(F32)
     order_column = column(order)[:, :n_lat]
     order_pick = jnp.where(
         order_column == iota((n_lat, n_lat), 1).astype(F32), 1.0, 0.0
@@ -162,19 +155,17 @@
     lax.fori_loop(0, n_rad - 1, send_matrices, 0)
     pltpu.make_async_copy(inverse_hbm.at[pl.ds(y * own, own)], matrices.at[:, y], recv0).start()
 
-    smalls[1].wait()
-    smalls[2].wait()
     mine = jnp.sum(jnp.where(iota((1, n_lat), 1) == me, order, 0.0), axis=1, keepdims=True)
     count = jnp.sum(
-        jnp.where(iota((1, n_lat), 1).astype(F32) == mine, count_ref[...].astype(F32), 0.0),
+        jnp.where(iota((1, n_lat), 1).astype(F32) == mine, small[0:1, n_lat:2 * n_lat].astype(F32), 0.0),
         axis=1, keepdims=True,
     )
     first = n_deg - count
-    blocks, block = degree_ref.shape
+    blocks, block = small.shape[0] - 1, small.shape[1]
 
     def to_column(b, carry):
         at = pl.ds(pl.multiple_of(b * block, block), block)
-        natural_degree[at, :] = column(degree_ref[pl.ds(b, 1), :].astype(F32))
+        natural_degree[at, :] = column(small[pl.ds(b + 1, 1), :].astype(F32))
         return carry
 
     lax.fori_loop(0, blocks, to_column, 0)
@@ -362,12 +353,10 @@
     solved = pl.pallas_call(
         functools.partial(kernel, (n_lat, n_rad, n_l, n_deg, n_t)),
         out_shape=jax.ShapeDtypeStruct((own, PIECES, n_rad, n_q // PIECES, c * n_lat), BF16),
-        in_specs=[any_space] * 6,
+        in_specs=[any_space] * 4,
         out_specs=any_space,
         scratch_shapes=[
-            pltpu.VMEM((1, n_lat), jnp.int32),
-            pltpu.VMEM((n_deg // block, block), jnp.int32),
-            pltpu.VMEM((1, n_lat), jnp.int32),
+            pltpu.VMEM((n_deg // block + 1, block), jnp.int32),
             pltpu.VMEM((n_l, f * c * r, h, m), BF16),
             pltpu.VMEM((n_deg, n_h), BF16),
             pltpu.VMEM((n_lat * n_l, LANES), F32),
@@ -386,17 +375,15 @@
             pltpu.VMEM((own, n_rad, n_q, full), BF16),
             pltpu.VMEM((own, PIECES, full, c * n_lat), BF16),
             pltpu.VMEM((own, PIECES, n_rad, n_q // PIECES, c * n_lat), BF16),
-            dma((3,)), dma((n_l,)), dma, dma, dma,
+            dma, dma((n_l,)), dma, dma, dma,
             dma, dma, dma((own,)), dma((own,)),
             dma((own, PIECES)), dma((own, PIECES)), dma((own, PIECES)), dma((own, PIECES)),
         ],
         compiler_params=pltpu.CompilerParams(
-            collective_id=0, has_side_effects=True, vmem_limit_bytes=56 << 20
+            collective_id=0, has_side_effects=True, vmem_limit_bytes=53 << 20
         ),
     )(
-        order_of_slot.reshape(1, n_lat),
-        degree_of_slot.reshape(n_deg // block, block),
-        degree_count.reshape(1, n_lat),
+        jnp.concatenate([order_of_slot, degree_count, degree_of_slot]).reshape(-1, block),
         rows,
         legendre.reshape(n_deg, n_h),
         inverse,
@@ -411,6 +398,7 @@
             )
         ],
         out_specs=pl.BlockSpec((n_rad, 1, n_q, c, n_lat), lambda i: (0, i, 0, 0, 0)),
+        compiler_params=pltpu.CompilerParams(vmem_limit_bytes=8 << 20),
     )(solved).reshape(n_t, n_q, c, n_lat)
 
 

time: 55.7 us -> 55.4 us (level)
  Pallas kernels: 55.3 us -> 54.5 us
  local copies, waits for them, and re-layouts: 0 us -> 0.79 us
    pallas_call x1, Pallas kernels: 2.07 us -> 1.18 us  [on_device(): pl.pallas_call(widen, grid=(own,), out_shape=jax.ShapeDtypeStruct((n_rad,...]
    concatenate x0 -> x1, local copies, waits for them, and re-layouts: none -> 0.79 us  [on_device(): jnp.concatenate([order_of_slot, degree_count, degree_of_slot])]
where the time goes in v6:
time: 55.4 us; the launch traced here: 55.3 us
  Pallas kernels  54.5 us (98%)
  local copies, waits for them, and re-layouts  0.79 us (1%)
    pallas_call x1, Pallas kernels, on_device(): pl.pallas_call(functools.partial(kernel, (n_lat, n_rad, n_l, n_deg, n_t))...  53.3 us
    pallas_call x1, Pallas kernels, on_device(): pl.pallas_call(widen, grid=(own,), out_shape=jax.ShapeDtypeStruct((n_rad,...  1.18 us

profile of v6, /device:TPU:1, one launch (start us, length us, event | category | flops | bytes accessed | tf_op | source)
XLA Modules:
  0.0 55.3 jit_solution(6420071051610413486)
XLA Ops:
  0.0 0.8 %concatenate.3 = s32[1152]{0:T(1024)S(1)} concatenate(s32[64]{0:T(128)} %param.9, s32[64]{0:T(128)} %param.11, s32[1024]{0:T(1024)} %param.10), dimensions={0} | concatenate | bytes 9216 | tf_op jit(solution)/shard_map/concatenate | solution.py:386
  0.8 53.3 %shard_map.64.solved_ref = bf16[2,2,8,32,128]{4,3,2,1,0:T(8,128)(2,1)S(1)} custom-call(s32[9,128]{1,0:T(8,128)S(1)} %bitcast.6, bf16[128,18,2,64]{3,2,1,0:T(2,128)(2,1)} %bitcast.8, bf16[1024,1152]{1,0:T(8,128)(2,1)} %bitcast.7, bf16[16,64,512]{2,1,0:T(8,128)(2,1)} %inverse_hbm.1), custom_call_target="tpu_custom_call" | custom-call | tf_op jit(solution)/shard_map/pallas_call | solution.py:353
  54.1 1.2 %shard_map.65 = f32[8,2,64,2,64]{4,3,2,1,0:T(2,128)} custom-call(bf16[2,2,8,32,128]{4,3,2,1,0:T(8,128)(2,1)S(1)} %shard_map.64.solved_ref), custom_call_target="tpu_custom_call" | custom-call | tf_op jit(solution)/shard_map/pallas_call | solution.py:391

commit v7 on v6

--- a/solution.py
+++ b/solution.py
@@ -273,15 +273,15 @@
                 got_c.at[h, p, others], got_c.at[h, p, others], recv3.at[h, p]
             ).wait()
             for o in range(n_rad):
-                block = got_c[h, p, o].astype(F32)
+                block = got_c[h, p, o]
                 turned = jnp.transpose(jnp.concatenate([block] * (2 * PIECES), axis=0))
                 for f in range(2):
                     at = 2 * f * radii
                     begin = f * (full // 2) + o * radii
                     right_side[h, p, begin:begin + radii, :] = jnp.where(
                         second_part,
-                        turned[at + radii:at + 2 * radii, :],
-                        turned[at:at + radii, :],
+                        turned[at + radii:at + 2 * radii, :].astype(F32),
+                        turned[at:at + radii, :].astype(F32),
                     ).astype(BF16)
             solved = jnp.dot(
                 matrices.at[h].reshape(full, full)[...], right_side[h, p],

time: 55.4 us -> 55.4 us (level)
  no operation moved by 1% of the time
where the time goes in v7:
time: 55.4 us; the launch traced here: 55.3 us
  Pallas kernels  54.5 us (98%)
  local copies, waits for them, and re-layouts  0.79 us (1%)
    pallas_call x1, Pallas kernels, on_device(): pl.pallas_call(functools.partial(kernel, (n_lat, n_rad, n_l, n_deg, n_t))...  53.3 us
    pallas_call x1, Pallas kernels, on_device(): pl.pallas_call(widen, grid=(own,), out_shape=jax.ShapeDtypeStruct((n_rad,...  1.18 us

profile of v7, /device:TPU:1, one launch (start us, length us, event | category | flops | bytes accessed | tf_op | source)
XLA Modules:
  0.0 55.3 jit_solution(6063907710862223450)
XLA Ops:
  0.0 0.8 %concatenate.3 = s32[1152]{0:T(1024)S(1)} concatenate(s32[64]{0:T(128)} %param.9, s32[64]{0:T(128)} %param.11, s32[1024]{0:T(1024)} %param.10), dimensions={0} | concatenate | bytes 9216 | tf_op jit(solution)/shard_map/concatenate | solution.py:386
  0.8 53.3 %shard_map.64.solved_ref = bf16[2,2,8,32,128]{4,3,2,1,0:T(8,128)(2,1)S(1)} custom-call(s32[9,128]{1,0:T(8,128)S(1)} %bitcast.6, bf16[128,18,2,64]{3,2,1,0:T(2,128)(2,1)} %bitcast.8, bf16[1024,1152]{1,0:T(8,128)(2,1)} %bitcast.7, bf16[16,64,512]{2,1,0:T(8,128)(2,1)} %inverse_hbm.1), custom_call_target="tpu_custom_call" | custom-call | tf_op jit(solution)/shard_map/pallas_call | solution.py:353
  54.1 1.2 %shard_map.65 = f32[8,2,64,2,64]{4,3,2,1,0:T(2,128)} custom-call(bf16[2,2,8,32,128]{4,3,2,1,0:T(8,128)(2,1)S(1)} %shard_map.64.solved_ref), custom_call_target="tpu_custom_call" | custom-call | tf_op jit(solution)/shard_map/pallas_call | solution.py:391

commit v8 on v7

--- a/solution.py
+++ b/solution.py
@@ -86,12 +86,14 @@
         )
         return carry
 
-    lax.fori_loop(0, planes - 1, greet_lat, 0)
+    for k in range(planes - 1):
+        greet_lat(k, 0)
     for place in places[:-1]:
         pl.semaphore_signal(
             barrier, inc=1, device_id={"lat": z * group + place}, device_id_type=MESH
         )
-    lax.fori_loop(1, n_rad, greet_rad, 0)
+    for k in range(1, n_rad):
+        greet_rad(k, 0)
 
     load_small.wait()
     order = small[0:1, :n_lat].astype(F32)

time: 55.4 us -> 55.5 us (level)
  no operation moved by 1% of the time
where the time goes in v8:
time: 55.5 us; the launch traced here: 55.4 us
  Pallas kernels  54.6 us (98%)
  local copies, waits for them, and re-layouts  0.79 us (1%)
    pallas_call x1, Pallas kernels, on_device(): pl.pallas_call(functools.partial(kernel, (n_lat, n_rad, n_l, n_deg, n_t))...  53.4 us
    pallas_call x1, Pallas kernels, on_device(): pl.pallas_call(widen, grid=(own,), out_shape=jax.ShapeDtypeStruct((n_rad,...  1.18 us

profile of v8, /device:TPU:1, one launch (start us, length us, event | category | flops | bytes accessed | tf_op | source)
XLA Modules:
  0.0 55.4 jit_solution(13947019869961361945)
XLA Ops:
  0.0 0.8 %concatenate.3 = s32[1152]{0:T(1024)S(1)} concatenate(s32[64]{0:T(128)} %param.9, s32[64]{0:T(128)} %param.11, s32[1024]{0:T(1024)} %param.10), dimensions={0} | concatenate | bytes 9216 | tf_op jit(solution)/shard_map/concatenate | solution.py:388
  0.8 53.4 %shard_map.64.solved_ref = bf16[2,2,8,32,128]{4,3,2,1,0:T(8,128)(2,1)S(1)} custom-call(s32[9,128]{1,0:T(8,128)S(1)} %bitcast.6, bf16[128,18,2,64]{3,2,1,0:T(2,128)(2,1)} %bitcast.8, bf16[1024,1152]{1,0:T(8,128)(2,1)} %bitcast.7, bf16[16,64,512]{2,1,0:T(8,128)(2,1)} %inverse_hbm.1), custom_call_target="tpu_custom_call" | custom-call | tf_op jit(solution)/shard_map/pallas_call | solution.py:355
  54.2 1.2 %shard_map.65 = f32[8,2,64,2,64]{4,3,2,1,0:T(2,128)} custom-call(bf16[2,2,8,32,128]{4,3,2,1,0:T(8,128)(2,1)S(1)} %shard_map.64.solved_ref), custom_call_target="tpu_custom_call" | custom-call | tf_op jit(solution)/shard_map/pallas_call | solution.py:393
